TPU v7x, 128 devices: a whole 4x4x4 slice. The times are simulated.
128 devices in a mesh: blk: 32 (over z, y, core), grp: 4 (over x).
Axes of the slice: x: 4, y: 4, z: 4, core: 2. Of those that a mesh axis runs over, the one named last changes fastest.
Arguments:
- block_inverse: bfloat16 [256, 1024, 1024], P(('blk', 'grp')), may hold values from -5 to 5
- coupling_in: bfloat16 [256, 1024, 1536], P(('blk', 'grp')), may hold values from -0.046875 to 0.046875
- coupling_out: bfloat16 [256, 1536, 1024], P(('blk', 'grp')), may hold values from -0.15625 to 0.15625
- sensitivities: bfloat16 [256, 1024, 512], P(('blk', 'grp')), may hold values from -6 to 6
- border_rhs: bfloat16 [1536, 512], replicated, may hold values from -6 to 6
- border_inverse: bfloat16 [1536, 1536], P('blk'), may hold values from -5 to 5
Outputs:
- adjoint: bfloat16 [256, 1024, 512], P(('blk', 'grp'))
- border_part: bfloat16 [1536, 512], P('blk')
All inputs are finite; a program needn't handle non-finite values.
Results may differ from a plain program's by a relative error of at most 0.0067.
Values may be sent and summed in bfloat16 or wider, within the bound.
No kernel may reach another device: no remote copies, remote signals or barrier semaphores. Data moves between devices by JAX's collectives and lax.ppermute only.
A program may use at most 128 MiB of HBM per device.

v0:
```python
import jax
import jax.numpy as jnp
from jax import lax
from jax.sharding import PartitionSpec as P


def body(block_inverse, coupling_in, coupling_out, sensitivities, border_rhs, border_inverse):
    forward_part = jnp.einsum(
        "bji,bjk->bik", block_inverse, sensitivities, preferred_element_type=jnp.float32
    )
    forward_half = forward_part.astype(jnp.bfloat16)
    row_count = border_inverse.shape[0]
    owner_index = lax.axis_index("blk")
    full_term = jnp.einsum(
        "bnm,bnk->mk", coupling_in, forward_half, preferred_element_type=jnp.float32
    )
    summed_all = lax.psum(full_term, ("blk", "grp"))
    residual_half = (border_rhs.astype(jnp.float32) - summed_all).astype(jnp.bfloat16)
    full_border = lax.dot_general(
        lax.all_gather(border_inverse, "blk", axis=0, tiled=True),
        residual_half,
        (((0,), (0,)), ((), ())),
        preferred_element_type=jnp.float32,
    ).astype(jnp.bfloat16)
    border_rows = lax.dynamic_slice_in_dim(full_border, owner_index * row_count, row_count, 0)
    pulled = jnp.einsum(
        "bmn,mk->bnk", coupling_out, full_border, preferred_element_type=jnp.float32
    ).astype(jnp.bfloat16)
    back_term = jnp.einsum(
        "bji,bjk->bik", block_inverse, pulled, preferred_element_type=jnp.float32
    )
    adjoint = (forward_part - back_term).astype(jnp.bfloat16)
    return (adjoint, border_rows)


def solution(mesh):
    in_specs = (
        P(("blk", "grp"), None, None),
        P(("blk", "grp"), None, None),
        P(("blk", "grp"), None, None),
        P(("blk", "grp"), None, None),
        P(),
        P("blk", None),
    )
    out_specs = (P(("blk", "grp"), None, None), P("blk", None))
    return jax.shard_map(body, mesh=mesh, in_specs=in_specs, out_specs=out_specs, check_vma=False)
```

profile of v0, /device:TPU:1, one launch (start us, length us, event | category | flops | bytes accessed | tf_op | source)
XLA Modules:
  0.0 209.8 jit_solution(1370069537564459499)
XLA Ops:
  8.0 0.0 copy-start
  8.0 0.0 all-reduce.2.cloned.1.call-start
  8.1 1.5 copy-done
  9.6 4.6 %fusion.10 = f32[2,1024,512]{2,1,0:T(8,128)S(1)} fusion(bf16[2,1024,1024]{2,1,0:T(8,128)(2,1)} %param.6, bf16[2,1024,512]{2,1,0:T(8,128)(2,1)S(1)} %copy-done), kind=kOutput, calls=%fused_computation.11 | convolution fusion | flops 2147483648 | bytes 10485760 | tf_op jit(solution)/shard_map/bji,bjk->bik/dot_general | solution.py:8
  14.2 0.0 copy-start.2
  14.2 2.0 copy-done.2
  16.2 8.0 %convolution_bitcast_fusion = f32[1536,512]{1,0:T(8,128)} fusion(bf16[2,1024,1536]{2,1,0:T(8,128)(2,1)} %param.7, f32[2,1024,512]{2,1,0:T(8,128)S(1)} %fusion.10), kind=kOutput, calls=%fused_computation.2 | convolution fusion | flops 3222274048 | bytes 13631488 | tf_op jit(solution)/shard_map/bnm,bnk->mk/dot_general | solution.py:14
  24.2 0.0 all-reduce.2.cloned.1.call-update
  24.2 0.2 all-gather.2.cloned.1.call-start
  24.4 0.3 all-gather.2.cloned.1.call-update
  24.8 156.6 %all-reduce.2.cloned.1.call-done = f32[1536,512]{1,0:T(8,128)} async-done(((f32[1536,512]{1,0:T(8,128)}), f32[1536,512]{1,0:T(8,128)}) %all-reduce.2.cloned.1.call-update) | async-done | bytes 3145744 | tf_op jit(solution)/shard_map/psum | solution.py:17
  181.3 0.0 all-gather.2.cloned.1.call-done
  181.4 6.5 %convolution_convert_fusion = bf16[512,1536]{1,0:T(8,128)(2,1)S(1)} fusion(bf16[1536,1536]{1,0:T(8,128)(2,1)} %all-gather.2.cloned.1.call-done, f32[1536,512]{1,0:T(8,128)} %all-reduce.2.cloned.1.call-done, bf16[1536,512]{1,0:T(8,128)(2,1)} %param.10), kind=kOutput, calls=%fused_computation.4 | convolution fusion | flops 2419064832 | bytes 11010048 | tf_op jit(solution)/shard_map/dot_general | solution.py:19
  187.8 0.0 copy-start.1
  187.8 1.1 copy-done.1
  189.0 0.1 dynamic-slice_bitcast_fusion
  189.1 0.7 copy.10
  189.8 12.6 %fusion = bf16[2,1024,512]{2,1,0:T(8,128)(2,1)} fusion(f32[2,1024,512]{2,1,0:T(8,128)} %copy-done.2, bf16[2,1024,1024]{2,1,0:T(8,128)(2,1)} %param.6, bf16[2,1536,1024]{2,1,0:T(8,128)(2,1)} %param.8, bf16[512,1536]{1,0:T(8,128)(2,1)} %copy-done.1), kind=kOutput, calls=%fused_computation.1 | convolution fusion | flops 5371854848 | bytes 18350080 | tf_op jit(solution)/shard_map/bji,bjk->bik/dot_general | solution.py:29
Async XLA Ops:
  8.0 1.6 copy-start
  8.0 173.3 %all-reduce.2.cloned.1.call-start = ((), (), s32[]{:S(2)}) async-start(), calls=%async_computation | async-start | bytes 6291456 | tf_op jit(solution)/shard_map/psum | solution.py:17
  14.2 2.0 copy-start.2
  24.2 157.1 %all-gather.2.cloned.1.call-start = ((), (), s32[]{:S(2)}) async-start(), calls=%async_computation.1 | async-start | bytes 4866048 | tf_op jit(solution)/shard_map/all_gather | solution.py:20
  187.8 1.2 copy-start.1
Sparse Core Ops, SparseCore 0:
  24.3 156.9 all-reduce.1
Sparse Core Ops, SparseCore 1:
  26.9 50.8 all-gather.1
where the time goes:
time: 210 us
  waiting for transfers between devices  157 us (75%)
  matrix products  31.6 us (15%)
  between operations  15.5 us (7%)
  local copies, waits for them, and re-layouts  5.53 us (3%)
    psum x1, waiting for transfers between devices, body(): summed_all = lax.psum(full_term, ('blk', 'grp'))  157 us
    dot_general x1, matrix products, body(): jnp.einsum('bji,bjk->bik', block_inverse, pulled, preferred_element_type=...  12.6 us
    dot_general x1, matrix products, body(): jnp.einsum('bnm,bnk->mk', coupling_in, forward_half, preferred_element_ty...  8 us
    dot_general x1, matrix products, body(): lax.dot_general(lax.all_gather(border_inverse, 'blk', axis=0, tiled=True)...  6.45 us
    unnamed x7, local copies, waits for them, and re-layouts  5.42 us
    dot_general x1, matrix products, body(): jnp.einsum('bji,bjk->bik', block_inverse, sensitivities, preferred_elemen...  4.56 us
  transfers between devices with their start and end apart: 2, of which 1 were waited for; matrix products, arithmetic and copies ran while one was open for 0% of the time, Pallas kernels for 0%

commit v1 on v0

v1 whole, which is shorter than its diff:
```python
import jax
import jax.numpy as jnp
from jax import lax
from jax.sharding import Mesh, PartitionSpec as P

F32 = jnp.float32
BF16 = jnp.bfloat16
CHIPS = ("z", "y", "xh", "xl")
SWAP = [(0, 1), (1, 0)]


def body(block_inverse, coupling_in, coupling_out, sensitivities, border_rhs, border_inverse):
    core = lax.axis_index("core")
    xl = lax.axis_index("xl")
    chip = lax.axis_index(CHIPS)
    blk = lax.axis_index(("z", "y", "core"))
    rows, link = border_inverse.shape
    cols = sensitivities.shape[2]
    half, quarter = link // 2, link // 4
    piece = cols // 64

    chunks = border_inverse.reshape(rows, 2, 2, quarter)
    chunks = lax.dynamic_index_in_dim(chunks, xl, 2, keepdims=False).swapaxes(0, 1)
    chunks = jnp.broadcast_to(chunks[None], (16, 2, rows, quarter)).reshape(32, rows, quarter)
    solve_cols = lax.all_to_all(chunks, ("z", "y", "core"), 0, 0, tiled=True).reshape(link, quarter)

    forward = jnp.einsum("bjk,bji->bki", sensitivities, block_inverse, preferred_element_type=F32)
    forward, = lax.optimization_barrier((forward,))
    term = jnp.einsum("bkn,bnm->km", forward.astype(BF16), coupling_in, preferred_element_type=F32)

    away = lax.dynamic_slice_in_dim(term, (1 - core) * half, half, 1).astype(BF16)
    mine = lax.dynamic_slice_in_dim(term, core * half, half, 1)
    mine = (mine + lax.ppermute(away, "core", SWAP).astype(F32)).astype(BF16)
    parts = lax.all_to_all(mine.reshape(64, piece, half), CHIPS, 0, 0, tiled=True)
    total = jnp.sum(parts.astype(F32), axis=0)

    pick = (lax.broadcasted_iota(jnp.int32, (piece, cols), 1) == chip * piece + lax.broadcasted_iota(jnp.int32, (piece, cols), 0)).astype(BF16)
    rhs_half = lax.dynamic_slice_in_dim(border_rhs, core * half, half, 0)
    rhs = lax.dot_general(pick, rhs_half, (((1,), (1,)), ((), ())), preferred_element_type=F32)
    residual = (rhs - total).astype(BF16)
    other = lax.ppermute(residual, "xl", SWAP)
    residual = jnp.where(xl == 0, jnp.concatenate([residual, other], 0), jnp.concatenate([other, residual], 0))
    other = lax.ppermute(residual, "core", SWAP)
    residual = jnp.where(core == 0, jnp.concatenate([residual, other], 1), jnp.concatenate([other, residual], 1))

    solved = jnp.dot(residual, solve_cols, preferred_element_type=F32).astype(BF16)
    spread = jnp.broadcast_to(solved[None], (64,) + solved.shape)
    got = lax.all_to_all(spread, CHIPS, 0, 0, tiled=True)
    own = got.reshape(32, 2, 2 * piece, quarter).swapaxes(1, 2).reshape(cols, half)
    other = lax.ppermute(own, "core", SWAP)
    border = jnp.where(core == 0, jnp.concatenate([own, other], 1), jnp.concatenate([other, own], 1))

    pulled = jnp.einsum("km,bmn->bkn", border, coupling_out, preferred_element_type=F32).astype(BF16)
    pulled, = lax.optimization_barrier((pulled,))
    back = jnp.einsum("bkj,bji->bki", pulled, block_inverse, preferred_element_type=F32)
    adjoint = (forward - back).astype(BF16)
    adjoint, = lax.optimization_barrier((adjoint,))
    adjoint = adjoint.swapaxes(1, 2)

    pick = (lax.broadcasted_iota(jnp.int32, (rows, link), 1) == blk * rows + lax.broadcasted_iota(jnp.int32, (rows, link), 0)).astype(BF16)
    border_rows = lax.dot_general(pick, border, (((1,), (1,)), ((), ())), preferred_element_type=F32).astype(BF16)
    return (adjoint, border_rows)


def solution(mesh):
    mesh = Mesh(mesh.devices.reshape(4, 4, 2, 2, 2), ("z", "y", "core", "xh", "xl"))
    every = ("z", "y", "core", "xh", "xl")
    blocks = P(every, None, None)
    lines = P(("z", "y", "core"), None)
    return jax.shard_map(
        body, mesh=mesh, in_specs=(blocks, blocks, blocks, blocks, P(), lines), out_specs=(blocks, lines), check_vma=False
    )
```

time: 210 us -> 118 us (0.56)
  waiting for transfers between devices: 157 us -> 33.4 us
  starting transfers between devices: 0.26 us -> 21.5 us
  blocking collectives: 0 us -> 20.1 us
  between operations: 15.5 us -> 0.79 us
  local copies, waits for them, and re-layouts: 5.53 us -> 9.58 us
  other arithmetic: 0 us -> 3.98 us
  matrix products: 31.6 us -> 28.3 us
    psum x1 -> x0, waiting for transfers between devices: 157 us -> none  [body(): summed_all = lax.psum(full_term, ('blk', 'grp'))]
    all_to_all x0 -> x2, waiting for transfers between devices: none -> 26.8 us  [the longest x1 14.9 us: body(): lax.all_to_all(mine.reshape(64, piece, half), CHIPS, 0, 0, tiled=True)]
    all_to_all x0 -> x1, blocking collectives: none -> 20.1 us  [body(): got = lax.all_to_all(spread, CHIPS, 0, 0, tiled=True)]
    all_to_all x0 -> x2, starting transfers between devices: none -> 16.7 us  [the longest x1 11.2 us: body(): lax.all_to_all(mine.reshape(64, piece, half), CHIPS, 0, 0, tiled=True)]
    ppermute x0 -> x4, waiting for transfers between devices: none -> 6.63 us  [the longest x1 2.55 us: body(): other = lax.ppermute(residual, 'xl', SWAP)]
    ppermute x0 -> x4, starting transfers between devices: none -> 4.8 us  [the longest x1 1.82 us: body(): other = lax.ppermute(own, 'core', SWAP)]
    dot_general x4 -> x7, matrix products: 31.6 us -> 28.3 us  [the longest x1 7.08 us: body(): jnp.einsum('km,bmn->bkn', border, coupling_out, preferred_element_type=F32)]
    reshape x0 -> x1, other arithmetic: none -> 2.69 us  [body(): mine.reshape(64, piece, half)]
  transfers between devices with their start and end apart: 2 -> 6, of which waited for: 1 -> 5; matrix products, arithmetic and copies ran while one was open for 0% -> 3% of each run, Pallas kernels for 0% -> 0%
where the time goes in v1:
time: 118 us
  waiting for transfers between devices  33.4 us (28%)
  matrix products  28.3 us (24%)
  starting transfers between devices  21.5 us (18%)
  blocking collectives  20.1 us (17%)
  local copies, waits for them, and re-layouts  9.58 us (8%)
  other arithmetic  3.98 us (3%)
    all_to_all x1, blocking collectives, body(): got = lax.all_to_all(spread, CHIPS, 0, 0, tiled=True)  20.1 us
    all_to_all x1, waiting for transfers between devices, body(): lax.all_to_all(mine.reshape(64, piece, half), CHIPS, 0, 0, tiled=True)  14.9 us
    all_to_all x1, waiting for transfers between devices, body(): lax.all_to_all(chunks, ('z', 'y', 'core'), 0, 0, tiled=True)  11.8 us
    all_to_all x1, starting transfers between devices, body(): lax.all_to_all(mine.reshape(64, piece, half), CHIPS, 0, 0, tiled=True)  11.2 us
    unnamed x14, local copies, waits for them, and re-layouts  7.37 us
    dot_general x1, matrix products, body(): jnp.einsum('km,bmn->bkn', border, coupling_out, preferred_element_type=F32)  7.08 us
    dot_general x1, matrix products, body(): jnp.einsum('bkn,bnm->km', forward.astype(BF16), coupling_in, preferred_el...  6.76 us
    dot_general x1, matrix products, body(): jnp.einsum('bjk,bji->bki', sensitivities, block_inverse, preferred_elemen...  6.51 us
  transfers between devices with their start and end apart: 6, of which 5 were waited for; matrix products, arithmetic and copies ran while one was open for 3% of the time, Pallas kernels for 0%

profile of v1, /device:TPU:1, one launch (start us, length us, event | category | flops | bytes accessed | tf_op | source)
XLA Modules:
  0.0 117.7 jit_solution(12457013789019274868)
XLA Ops:
  0.6 0.0 copy-start
  0.7 1.6 %copy-done = bf16[2,1024,512]{2,1,0:T(8,128)(2,1)S(1)} copy-done((bf16[2,1024,512]{2,1,0:T(8,128)(2,1)S(1)}, bf16[2,1024,512]{2,1,0:T(8,128)(2,1)}, u32[]{:S(2)}) %copy-start) | copy-done | bytes 2097176
  2.2 6.5 %fusion.17 = f32[2,512,1024]{2,1,0:T(8,128)} fusion(bf16[2,1024,512]{2,1,0:T(8,128)(2,1)S(1)} %copy-done, bf16[2,1024,1024]{2,1,0:T(8,128)(2,1)} %param.6), kind=kOutput, calls=%fused_computation.35 | convolution fusion | flops 2147483648 | bytes 10485760 | tf_op jit(solution)/shard_map/bjk,bji->bki/dot_general | solution.py:27
  8.7 6.8 %convolution_bitcast_fusion = f32[512,1536]{1,0:T(8,128)S(1)} fusion(bf16[2,1024,1536]{2,1,0:T(8,128)(2,1)} %param.7, f32[2,512,1024]{2,1,0:T(8,128)} %fusion.17), kind=kOutput, calls=%fused_computation.1 | convolution fusion | flops 3222274048 | bytes 13631488 | tf_op jit(solution)/shard_map/bkn,bnm->km/dot_general | solution.py:29
  15.5 0.0 copy-start.2
  15.5 1.7 %copy-done.2 = f32[512,1536]{1,0:T(8,128)} copy-done((f32[512,1536]{1,0:T(8,128)}, f32[512,1536]{1,0:T(8,128)S(1)}, u32[]{:S(2)}) %copy-start.2) | copy-done | bytes 3145752
  17.2 0.1 dynamic-slice_convert_fusion
  17.3 1.5 %collective-permute-start = (bf16[512,768]{1,0:T(8,128)(2,1)S(1)}, bf16[512,768]{1,0:T(8,128)(2,1)}, u32[]{:S(2)}, u32[]{:S(2)}) collective-permute-start(bf16[512,768]{1,0:T(8,128)(2,1)S(1)} %dynamic-slice_convert_fusion), channel_id=1, source_target_pairs={{0,4},{4,0},{1,5},{5,1},{2,6},{6,2},{3,7},{7,3},{8,12},{12,8},{9,1... | collective-permute-start | bytes 2359304 | tf_op jit(solution)/shard_map/ppermute | solution.py:33
  18.7 0.0 copy-start.3
  18.7 2.0 %collective-permute-done = bf16[512,768]{1,0:T(8,128)(2,1)} collective-permute-done((bf16[512,768]{1,0:T(8,128)(2,1)S(1)}, bf16[512,768]{1,0:T(8,128)(2,1)}, u32[]{:S(2)}, u32[]{:S(2)}) %collective-permute-start) | collective-permute-done | bytes 786464 | tf_op jit(solution)/shard_map/ppermute | solution.py:33
  20.8 2.7 %fusion.3 = bf16[64,8,768]{2,1,0:T(8,128)(2,1)} fusion(bf16[512,768]{1,0:T(8,128)(2,1)} %collective-permute-done, f32[512,1536]{1,0:T(8,128)} %copy-done.2, s32[]{:T(128)S(6)} %select_n.38), kind=kLoop, calls=%fused_computation.13 | loop fusion | flops 1179648 | bytes 3145732 | tf_op jit(solution)/shard_map/reshape | solution.py:34
  23.5 11.2 %all-to-all-start = ((bf16[64,8,768]{2,1,0:T(8,128)(2,1)}), bf16[64,8,768]{2,1,0:T(8,128)(2,1)S(1)}, u32[]{:S(2)}, u32[]{:S(2)}) async-start(bf16[64,8,768]{2,1,0:T(8,128)(2,1)} %fusion.3), calls=%async_computation | async-start | bytes 1572864 | tf_op jit(solution)/shard_map/all_to_all | solution.py:34
  34.7 0.0 copy-done.3
  34.8 0.2 constant_dynamic-slice_fusion
  35.0 14.9 %all-to-all-done = bf16[64,8,768]{2,1,0:T(8,128)(2,1)S(1)} async-done(((bf16[64,8,768]{2,1,0:T(8,128)(2,1)}), bf16[64,8,768]{2,1,0:T(8,128)(2,1)S(1)}, u32[]{:S(2)}, u32[]{:S(2)}) %all-to-all-start) | async-done | bytes 786464 | tf_op jit(solution)/shard_map/all_to_all | solution.py:34
  49.9 0.0 copy-start.1
  49.9 1.2 %broadcast_in_dim.4 = bf16[16,2,48,384]{3,2,1,0:T(8,128)(2,1)} broadcast(bf16[2,48,384]{2,1,0:T(8,128)(2,1)S(1)} %bitcast.38), dimensions={1,2,3} | broadcast | bytes 1253376 | tf_op jit(solution)/shard_map/broadcast_in_dim | solution.py:24
  51.1 0.0 copy-done.1
  51.2 5.5 %all-to-all-start.1 = ((bf16[32,48,384]{2,1,0:T(8,128)(2,1)}), bf16[32,48,384]{2,1,0:T(8,128)(2,1)S(1)}, u32[]{:S(2)}, u32[]{:S(2)}) async-start(bf16[32,48,384]{2,1,0:T(8,128)(2,1)} %bitcast.31), calls=%async_computation.1 | async-start | bytes 2359296 | tf_op jit(solution)/shard_map/all_to_all | solution.py:25
  56.7 1.3 %convert_reduce_fusion = f32[8,768]{1,0:T(8,128)S(1)} fusion(bf16[64,8,768]{2,1,0:T(8,128)(2,1)} %copy-done.1), kind=kLoop, calls=%fused_computation.6 | loop fusion | flops 780288 | bytes 811008 | tf_op jit(solution)/shard_map/reduce_sum | solution.py:35
  58.0 1.4 %fusion.2 = bf16[8,768]{1,0:T(8,128)(2,1)S(1)} fusion(f32[8,768]{1,0:T(8,128)S(1)} %convert_reduce_fusion, bf16[1536,512]{1,0:T(8,128)(2,1)} %param.10, s32[]{:T(128)S(6)} %select_n.38, s32[8]{0:T(128)S(1)} %iota_add_fusion.1), kind=kOutput, calls=%fused_computation.11 | convolution fusion | flops 6307840 | bytes 823332 | tf_op jit(solution)/shard_map/dot_general | solution.py:39
  59.4 0.3 collective-permute-start.1
  59.7 2.5 %collective-permute-done.1 = bf16[8,768]{1,0:T(8,128)(2,1)S(1)} collective-permute-done((bf16[8,768]{1,0:T(8,128)(2,1)S(1)}, bf16[8,768]{1,0:T(8,128)(2,1)S(1)}, u32[]{:S(2)}, u32[]{:S(2)}) %collective-permute-start.1) | collective-permute-done | bytes 12320 | tf_op jit(solution)/shard_map/ppermute | solution.py:41
  62.3 1.2 %collective-permute-start.2 = (bf16[16,768]{1,0:T(8,128)(2,1)S(1)}, bf16[16,768]{1,0:T(8,128)(2,1)S(1)}, u32[]{:S(2)}, u32[]{:S(2)}) collective-permute-start(bf16[16,768]{1,0:T(8,128)(2,1)S(1)} %maximum_select_fusion.5), channel_id=1, source_target_pairs={{0,4},{4,0},{1,5},{5,1},{2,6},{6,2},{3,7},{7,3},{8,12},{12,8},{9,1... | collective-permute-start | bytes 73736 | tf_op jit(solution)/shard_map/ppermute | solution.py:43
  63.5 11.8 %all-to-all-done.1 = bf16[32,48,384]{2,1,0:T(8,128)(2,1)S(1)} async-done(((bf16[32,48,384]{2,1,0:T(8,128)(2,1)}), bf16[32,48,384]{2,1,0:T(8,128)(2,1)S(1)}, u32[]{:S(2)}, u32[]{:S(2)}) %all-to-all-start.1) | async-done | bytes 1179680 | tf_op jit(solution)/shard_map/all_to_all | solution.py:25
  75.3 0.0 collective-permute-done.2
  75.3 0.3 convolution_convert_fusion.1
  75.6 0.1 broadcast_in_dim.5
  75.7 20.1 %all_to_all.15 = bf16[64,16,384]{2,1,0:T(8,128)(2,1)S(1)} all-to-all(bf16[64,16,384]{2,1,0:T(8,128)(2,1)S(1)} %broadcast_in_dim.5), channel_id=1, replica_groups=mesh['z'=4,'y'=4,'core'=2,'xh'=2,'xl'=2] {'z','y','xh','xl'}, dimensions={0} | all-to-all | bytes 1572864 | tf_op jit(solution)/shard_map/all_to_all | solution.py:48
  95.8 0.6 copy.14
  96.4 0.1 copy.17
  96.5 1.8 %collective-permute-start.3 = (bf16[512,768]{1,0:T(8,128)(2,1)S(1)}, bf16[512,768]{1,0:T(8,128)(2,1)}, u32[]{:S(2)}, u32[]{:S(2)}) collective-permute-start(bf16[512,768]{1,0:T(8,128)(2,1)S(1)} %bitcast.35), channel_id=1, source_target_pairs={{0,4},{4,0},{1,5},{5,1},{2,6},{6,2},{3,7},{7,3},{8,12},{12,8},{9,1... | collective-permute-start | bytes 2359304 | tf_op jit(solution)/shard_map/ppermute | solution.py:50
  98.4 0.0 copy-start.4
  98.4 0.0 copy-start.5
  98.4 2.0 %collective-permute-done.3 = bf16[512,768]{1,0:T(8,128)(2,1)} collective-permute-done((bf16[512,768]{1,0:T(8,128)(2,1)S(1)}, bf16[512,768]{1,0:T(8,128)(2,1)}, u32[]{:S(2)}, u32[]{:S(2)}) %collective-permute-start.3) | collective-permute-done | bytes 786464 | tf_op jit(solution)/shard_map/ppermute | solution.py:50
  100.4 7.1 %convert_bitcast_fusion = bf16[2,512,1024]{2,1,0:T(8,128)(2,1)S(1)} fusion(bf16[2,1536,1024]{2,1,0:T(8,128)(2,1)} %param.8, bf16[512,768]{1,0:T(8,128)(2,1)} %collective-permute-done.3, bf16[512,768]{1,0:T(8,128)(2,1)S(1)} %bitcast.36, pred[]{:T(512)S(6)} %eq.13), kind=kOutput, calls=%fused_computation.2 | convolution fusion | flops 3229351936 | bytes 9961473 | tf_op jit(solution)/shard_map/km,bmn->bkn/dot_general | solution.py:53
  107.5 0.0 copy-done.4
  107.5 0.0 copy-done.5
  107.5 3.7 %subtract_convert_fusion = bf16[2,512,1024]{2,1,0:T(8,128)(2,1)} fusion(f32[2,512,1024]{2,1,0:T(8,128)S(1)} %copy-done.5, bf16[2,512,1024]{2,1,0:T(8,128)(2,1)S(1)} %convert_bitcast_fusion, bf16[2,1024,1024]{2,1,0:T(8,128)(2,1)S(1)} %copy-done.4), kind=kOutput, calls=%fused_computation | convolution fusion | flops 2149580800 | bytes 12582912 | tf_op jit(solution)/shard_map/bkj,bji->bki/dot_general | solution.py:55
  111.2 3.9 %copy.15 = bf16[2,1024,512]{2,1,0:T(8,128)(2,1)} copy(bf16[2,1024,512]{1,2,0:T(8,128)(2,1)} %bitcast.34) | data formatting | bytes 4194304
  115.2 2.6 %convolution_convert_fusion = bf16[48,512]{1,0:T(8,128)(2,1)} fusion(bf16[512,768]{1,0:T(8,128)(2,1)} %collective-permute-done.3, bf16[512,768]{1,0:T(8,128)(2,1)S(1)} %bitcast.37, pred[]{:T(512)S(6)} %eq.13, s32[48]{0:T(128)S(1)} %iota_add_fusion), kind=kOutput, calls=%fused_computation.9 | convolution fusion | flops 82673664 | bytes 1622209 | tf_op jit(solution)/shard_map/dot_general | solution.py:61
  (5 shorter events, 0.1 us)
Async XLA Ops:
  0.6 1.6 %copy-start = (bf16[2,1024,512]{2,1,0:T(8,128)(2,1)S(1)}, bf16[2,1024,512]{2,1,0:T(8,128)(2,1)}, u32[]{:S(2)}) copy-start(bf16[2,1024,512]{2,1,0:T(8,128)(2,1)} %param.9) | copy-start | bytes 6291460
  15.5 1.7 %copy-start.2 = (f32[512,1536]{1,0:T(8,128)}, f32[512,1536]{1,0:T(8,128)S(1)}, u32[]{:S(2)}) copy-start(f32[512,1536]{1,0:T(8,128)S(1)} %convolution_bitcast_fusion) | copy-start | bytes 9437188
  17.3 3.5 %collective-permute-start = (bf16[512,768]{1,0:T(8,128)(2,1)S(1)}, bf16[512,768]{1,0:T(8,128)(2,1)}, u32[]{:S(2)}, u32[]{:S(2)}) collective-permute-start(bf16[512,768]{1,0:T(8,128)(2,1)S(1)} %dynamic-slice_convert_fusion), channel_id=1, source_target_pairs={{0,4},{4,0},{1,5},{5,1},{2,6},{6,2},{3,7},{7,3},{8,12},{12,8},{9,1... | collective-permute-start | bytes 2359304 | tf_op jit(solution)/shard_map/ppermute | solution.py:33
  18.7 16.0 %copy-start.3 = (bf16[48,1536]{1,0:T(8,128)(2,1)S(1)}, bf16[48,1536]{1,0:T(8,128)(2,1)}, u32[]{:S(2)}) copy-start(bf16[48,1536]{1,0:T(8,128)(2,1)} %param.11) | copy-start | bytes 442372
  23.5 26.4 %all-to-all-start = ((bf16[64,8,768]{2,1,0:T(8,128)(2,1)}), bf16[64,8,768]{2,1,0:T(8,128)(2,1)S(1)}, u32[]{:S(2)}, u32[]{:S(2)}) async-start(bf16[64,8,768]{2,1,0:T(8,128)(2,1)} %fusion.3), calls=%async_computation | async-start | bytes 1572864 | tf_op jit(solution)/shard_map/all_to_all | solution.py:34
  49.9 1.3 %copy-start.1 = (bf16[64,8,768]{2,1,0:T(8,128)(2,1)}, bf16[64,8,768]{2,1,0:T(8,128)(2,1)S(1)}, u32[]{:S(2)}) copy-start(bf16[64,8,768]{2,1,0:T(8,128)(2,1)S(1)} %all-to-all-done) | copy-start | bytes 2359300
  51.2 24.1 %all-to-all-start.1 = ((bf16[32,48,384]{2,1,0:T(8,128)(2,1)}), bf16[32,48,384]{2,1,0:T(8,128)(2,1)S(1)}, u32[]{:S(2)}, u32[]{:S(2)}) async-start(bf16[32,48,384]{2,1,0:T(8,128)(2,1)} %bitcast.31), calls=%async_computation.1 | async-start | bytes 2359296 | tf_op jit(solution)/shard_map/all_to_all | solution.py:25
  59.4 2.9 %collective-permute-start.1 = (bf16[8,768]{1,0:T(8,128)(2,1)S(1)}, bf16[8,768]{1,0:T(8,128)(2,1)S(1)}, u32[]{:S(2)}, u32[]{:S(2)}) collective-permute-start(bf16[8,768]{1,0:T(8,128)(2,1)S(1)} %fusion.2), channel_id=1, source_target_pairs={{0,1},{1,0},{2,3},{3,2},{4,5},{5,4},{6,7},{7,6},{8,9},{9,8},{10,11... | collective-permute-start | bytes 36872 | tf_op jit(solution)/shard_map/ppermute | solution.py:41
  62.3 13.0 %collective-permute-start.2 = (bf16[16,768]{1,0:T(8,128)(2,1)S(1)}, bf16[16,768]{1,0:T(8,128)(2,1)S(1)}, u32[]{:S(2)}, u32[]{:S(2)}) collective-permute-start(bf16[16,768]{1,0:T(8,128)(2,1)S(1)} %maximum_select_fusion.5), channel_id=1, source_target_pairs={{0,4},{4,0},{1,5},{5,1},{2,6},{6,2},{3,7},{7,3},{8,12},{12,8},{9,1... | collective-permute-start | bytes 73736 | tf_op jit(solution)/shard_map/ppermute | solution.py:43
  96.5 3.9 %collective-permute-start.3 = (bf16[512,768]{1,0:T(8,128)(2,1)S(1)}, bf16[512,768]{1,0:T(8,128)(2,1)}, u32[]{:S(2)}, u32[]{:S(2)}) collective-permute-start(bf16[512,768]{1,0:T(8,128)(2,1)S(1)} %bitcast.35), channel_id=1, source_target_pairs={{0,4},{4,0},{1,5},{5,1},{2,6},{6,2},{3,7},{7,3},{8,12},{12,8},{9,1... | collective-permute-start | bytes 2359304 | tf_op jit(solution)/shard_map/ppermute | solution.py:50
  98.4 9.1 %copy-start.4 = (bf16[2,1024,1024]{2,1,0:T(8,128)(2,1)S(1)}, bf16[2,1024,1024]{2,1,0:T(8,128)(2,1)}, u32[]{:S(2)}) copy-start(bf16[2,1024,1024]{2,1,0:T(8,128)(2,1)} %param.6) | copy-start | bytes 12582916
  98.4 9.1 %copy-start.5 = (f32[2,512,1024]{2,1,0:T(8,128)S(1)}, f32[2,512,1024]{2,1,0:T(8,128)}, u32[]{:S(2)}) copy-start(f32[2,512,1024]{2,1,0:T(8,128)} %fusion.17) | copy-start | bytes 12582916

commit v2 on v1

v2 whole, which is shorter than its diff:
```python
import jax
import jax.numpy as jnp
from jax import lax
from jax.experimental import pallas as pl
from jax.experimental.pallas import tpu as pltpu
from jax.sharding import Mesh, PartitionSpec as P

F32 = jnp.float32
BF16 = jnp.bfloat16
CHIPS = ("z", "y", "xh", "xl")
SWAP = [(0, 1), (1, 0)]
HBM = pl.BlockSpec(memory_space=pltpu.HBM)
VMEM = pl.BlockSpec(memory_space=pltpu.VMEM)


def params(mib):
    return pltpu.CompilerParams(vmem_limit_bytes=mib << 20)


def dot(a, b):
    return jnp.dot(a, b, preferred_element_type=F32)


def front_kernel(sens_hbm, inv_hbm, coup_hbm, fwd_hbm, fwd_half, away, coup_mine, fwd, inv, sens, coup_away, sems, out_sems):
    half = away.shape[1]
    core = lax.axis_index("core")
    copies = []
    for b in range(2):
        copies.append(pltpu.make_async_copy(sens_hbm.at[b], sens.at[b], sems.at[len(copies)]))
        copies.append(pltpu.make_async_copy(inv_hbm.at[b], inv.at[b], sems.at[len(copies)]))
    for b in range(2):
        lanes = pl.ds(pl.multiple_of((1 - core) * half, 128), half)
        copies.append(pltpu.make_async_copy(coup_hbm.at[b, :, lanes], coup_away.at[b], sems.at[len(copies)]))
    for b in range(2):
        lanes = pl.ds(pl.multiple_of(core * half, 128), half)
        copies.append(pltpu.make_async_copy(coup_hbm.at[b, :, lanes], coup_mine.at[b], sems.at[len(copies)]))
    outs = [pltpu.make_async_copy(fwd.at[b], fwd_hbm.at[b], out_sems.at[b]) for b in range(2)]
    for copy in copies:
        copy.start()
    for b in range(2):
        copies[2 * b].wait()
        turned = sens[b].T
        copies[2 * b + 1].wait()
        value = dot(turned, inv[b])
        fwd[b] = value
        outs[b].start()
        fwd_half[b] = value.astype(BF16)
    copies[4].wait()
    copies[5].wait()
    away[...] = (dot(fwd_half[0], coup_away[0]) + dot(fwd_half[1], coup_away[1])).astype(BF16)
    copies[6].wait()
    copies[7].wait()
    outs[0].wait()
    outs[1].wait()


def front(sens, inv, coup):
    n, k, m = inv.shape[1], sens.shape[2], coup.shape[2]
    return pl.pallas_call(
        front_kernel,
        name="front",
        out_shape=(
            pltpu.HBM((2, k, n), F32),
            pltpu.VMEM((2, k, n), BF16),
            pltpu.VMEM((k, m // 2), BF16),
            pltpu.VMEM((2, n, m // 2), BF16),
        ),
        in_specs=[HBM] * 3,
        out_specs=[HBM] + [VMEM] * 3,
        scratch_shapes=[
            pltpu.VMEM((2, k, n), F32),
            pltpu.VMEM((2, n, n), BF16),
            pltpu.VMEM((2, n, k), BF16),
            pltpu.VMEM((2, n, m // 2), BF16),
            pltpu.SemaphoreType.DMA((8,)),
            pltpu.SemaphoreType.DMA((2,)),
        ],
        compiler_params=params(30),
        cost_estimate=pl.CostEstimate(flops=2 * 2 * n * k * (n + m // 2), bytes_accessed=13 << 20, transcendentals=0),
    )(hb(sens), hb(inv), hb(coup))


def mine_kernel(fwd_half, coup_mine, out):
    out[...] = dot(fwd_half[0], coup_mine[0]) + dot(fwd_half[1], coup_mine[1])


def mine_half(fwd_half, coup_mine):
    k, m = fwd_half.shape[1], coup_mine.shape[2]
    return pl.pallas_call(
        mine_kernel,
        name="mine",
        out_shape=pltpu.VMEM((k, m), F32),
        in_specs=[VMEM] * 2,
        out_specs=VMEM,
        compiler_params=params(8),
        cost_estimate=pl.CostEstimate(flops=4 * k * m * fwd_half.shape[2], bytes_accessed=6 << 20, transcendentals=0),
    )(vm(fwd_half), vm(coup_mine))


def vm(x):
    return pltpu.with_memory_space_constraint(x, pltpu.VMEM)


def hb(x):
    return pltpu.with_memory_space_constraint(x, pltpu.HBM)


def pull_own_kernel(got, coup_hbm, out, coup_other, coup, sems):
    quarter = got.shape[3]
    half = 2 * quarter
    core = lax.axis_index("core")
    own = pl.ds(pl.multiple_of(core * half, 128), half)
    far = pl.ds(pl.multiple_of((1 - core) * half, 128), half)
    copies = [pltpu.make_async_copy(coup_hbm.at[b, own, :], coup.at[b], sems.at[b]) for b in range(2)]
    copies += [pltpu.make_async_copy(coup_hbm.at[b, far, :], coup_other.at[b], sems.at[2 + b]) for b in range(2)]
    for copy in copies:
        copy.start()
    lhs = [got[:, q].reshape(-1, quarter) for q in range(2)]
    for b in range(2):
        copies[b].wait()
        out[b] = dot(lhs[0], coup[b, :quarter, :]) + dot(lhs[1], coup[b, quarter:, :])
    copies[2].wait()
    copies[3].wait()


def pull_own(got, coup):
    k, m, n = got.shape[0] * got.shape[2], coup.shape[1], coup.shape[2]
    return pl.pallas_call(
        pull_own_kernel,
        name="pull_own",
        out_shape=(pltpu.VMEM((2, k, n), F32), pltpu.VMEM((2, m // 2, n), BF16)),
        in_specs=[VMEM, HBM],
        out_specs=[VMEM] * 2,
        scratch_shapes=[pltpu.VMEM((2, m // 2, n), BF16), pltpu.SemaphoreType.DMA((4,))],
        compiler_params=params(16),
        cost_estimate=pl.CostEstimate(flops=2 * k * n * m, bytes_accessed=8 << 20, transcendentals=0),
    )(vm(got), hb(coup))


def back_kernel(own, other, part, coup, inv_hbm, fwd_hbm, adjoint_hbm, border_hbm, inv, fwd, adjoint, border, sems):
    quarter = own.shape[3]
    core = lax.axis_index("core")
    zed = lax.axis_index("z")
    loads = []
    for b in range(2):
        loads.append(pltpu.make_async_copy(inv_hbm.at[b], inv.at[b], sems.at[3 + 2 * b]))
        loads.append(pltpu.make_async_copy(fwd_hbm.at[b], fwd.at[b], sems.at[4 + 2 * b]))
    for copy in loads:
        copy.start()
    lhs = [other[:, q].reshape(-1, quarter) for q in range(2)]
    copies = [pltpu.make_async_copy(adjoint.at[b], adjoint_hbm.at[b], sems.at[b]) for b in range(2)]
    copies.append(pltpu.make_async_copy(border, border_hbm, sems.at[2]))

    rows = border.shape[0]
    first = (lax.axis_index("y") * 2 + core) * rows
    spot = first + lax.broadcasted_iota(jnp.int32, (rows, quarter), 0)
    pick = (lax.broadcasted_iota(jnp.int32, (rows, quarter), 1) == spot).astype(BF16)

    def choose(ref):
        picked = ref[:, pl.ds(lax.rem(zed, 2), 1)].reshape(-1, quarter)
        border[...] = lax.dot_general(pick, picked, (((1,), (1,)), ((), ())), preferred_element_type=F32).astype(BF16)

    @pl.when(zed // 2 == core)
    def _():
        choose(own)

    @pl.when(zed // 2 != core)
    def _():
        choose(other)

    copies[2].start()
    for b in range(2):
        pulled = part[b] + dot(lhs[0], coup[b, :quarter, :]) + dot(lhs[1], coup[b, quarter:, :])
        loads[2 * b].wait()
        value = dot(pulled.astype(BF16), inv[b])
        loads[2 * b + 1].wait()
        adjoint[b] = (fwd[b] - value).astype(BF16).T
        copies[b].start()
    for copy in copies:
        copy.wait()


def backward(own, other, part, coup, inv, fwd, rows):
    _, k, n = part.shape
    return pl.pallas_call(
        back_kernel,
        name="back",
        out_shape=(jax.ShapeDtypeStruct((2, n, k), BF16), jax.ShapeDtypeStruct((rows, k), BF16)),
        in_specs=[VMEM] * 4 + [HBM] * 2,
        out_specs=[HBM] * 2,
        scratch_shapes=[
            pltpu.VMEM((2, n, n), BF16),
            pltpu.VMEM((2, k, n), F32),
            pltpu.VMEM((2, n, k), BF16),
            pltpu.VMEM((rows, k), BF16),
            pltpu.SemaphoreType.DMA((7,)),
        ],
        compiler_params=params(24),
        cost_estimate=pl.CostEstimate(flops=4 * k * n * (n + coup.shape[1]), bytes_accessed=20 << 20, transcendentals=0),
    )(vm(own), vm(other), vm(part), vm(coup), hb(inv), hb(fwd))


def steps(block_inverse, coupling_in, coupling_out, sensitivities, border_rhs, border_inverse):
    core = lax.axis_index("core")
    xl = lax.axis_index("xl")
    chip = lax.axis_index(CHIPS)
    rows, link = border_inverse.shape
    cols = sensitivities.shape[2]
    half, quarter = link // 2, link // 4
    piece = cols // 64

    chunks = jnp.where(xl == 0,
        jnp.stack([border_inverse[:, :quarter], border_inverse[:, 2 * quarter:3 * quarter]]),
        jnp.stack([border_inverse[:, quarter:2 * quarter], border_inverse[:, 3 * quarter:]]))
    chunks = jnp.broadcast_to(chunks[None], (16, 2, rows, quarter)).reshape(32, rows, quarter)
    solve_cols = lax.all_to_all(chunks, ("z", "y", "core"), 0, 0, tiled=True).reshape(link, quarter)

    fwd, fwd_half, away, coup_mine = front(sensitivities, block_inverse, coupling_in)
    came = lax.ppermute(away, "core", SWAP)
    mine = mine_half(fwd_half, coup_mine)
    mine = (mine + came.astype(F32)).astype(BF16)
    parts = lax.all_to_all(mine.reshape(64, piece, half), CHIPS, 0, 0, tiled=True)
    total = jnp.sum(parts.astype(F32), axis=0)

    pick = (lax.broadcasted_iota(jnp.int32, (piece, cols), 1) == chip * piece + lax.broadcasted_iota(jnp.int32, (piece, cols), 0)).astype(BF16)
    rhs_half = lax.dynamic_slice_in_dim(border_rhs, core * half, half, 0)
    rhs = lax.dot_general(pick, rhs_half, (((1,), (1,)), ((), ())), preferred_element_type=F32)
    residual = (rhs - total).astype(BF16)
    other = lax.ppermute(residual, "xl", SWAP)
    residual = jnp.where(xl == 0, jnp.concatenate([residual, other], 0), jnp.concatenate([other, residual], 0))
    other = lax.ppermute(residual, "core", SWAP)
    residual = jnp.where(core == 0, jnp.concatenate([residual, other], 1), jnp.concatenate([other, residual], 1))

    solved = dot(residual, solve_cols).astype(BF16)
    spread = jnp.broadcast_to(solved[None], (64,) + solved.shape)
    got = lax.all_to_all(spread, CHIPS, 0, 0, tiled=True)
    own = got.reshape(32, 2, 2 * piece, quarter)
    other = lax.ppermute(got, "core", SWAP).reshape(own.shape)
    part, coup_other = pull_own(own, coupling_out)
    return backward(own, other, part, coup_other, block_inverse, fwd, rows)


def solution(mesh):
    mesh = Mesh(mesh.devices.reshape(4, 4, 2, 2, 2), ("z", "y", "core", "xh", "xl"))
    every = ("z", "y", "core", "xh", "xl")
    blocks = P(every, None, None)
    lines = P(("z", "y", "core"), None)
    return jax.shard_map(
        steps, mesh=mesh, in_specs=(blocks, blocks, blocks, blocks, P(), lines), out_specs=(blocks, lines), check_vma=False
    )
```

time: 118 us -> 98.1 us (0.83)
  matrix products: 28.3 us -> 0.58 us
  Pallas kernels: 0 us -> 20.4 us
  local copies, waits for them, and re-layouts: 9.58 us -> 1.23 us
  other arithmetic: 3.98 us -> 1.22 us
  waiting for transfers between devices: 33.4 us -> 31.9 us
    dot_general x7 -> x2, matrix products: 28.3 us -> 0.58 us  [the longest x1 0.31 us: steps(): lax.dot_general(pick, rhs_half, (((1,), (1,)), ((), ())), preferred_eleme...]
    pallas_call x0 -> x4, Pallas kernels: none -> 20.4 us  [the longest x1 7.8 us: front(): pl.pallas_call(front_kernel, name='front', out_shape=(pltpu.HBM((2, k, n)...]
    unnamed x14 -> x4, local copies, waits for them, and re-layouts: 7.37 us -> 0.01 us
    ppermute x4, waiting for transfers between devices: 6.63 us -> 2.68 us  [the longest x1 2.55 us: steps(): other = lax.ppermute(residual, 'xl', SWAP)]
    all_to_all x2, waiting for transfers between devices: 26.8 us -> 29.2 us  [the longest x1 15.1 us: steps(): lax.all_to_all(mine.reshape(64, piece, half), CHIPS, 0, 0, tiled=True)]
    reshape x1, other arithmetic: 2.69 us -> 1.05 us  [steps(): mine.reshape(64, piece, half)]
  transfers between devices with their start and end apart: 6 -> 6, of which waited for: 5 -> 4; matrix products, arithmetic and copies ran while one was open for 3% -> 1% of each run, Pallas kernels for 0% -> 6%
where the time goes in v2:
time: 98.1 us; the launch traced here: 97.8 us
  waiting for transfers between devices  31.9 us (33%)
  starting transfers between devices  21.4 us (22%)
  Pallas kernels  20.4 us (21%)
  blocking collectives  20.1 us (20%)
  local copies, waits for them, and re-layouts  1.23 us (1%)
  other arithmetic  1.22 us (1%)
    all_to_all x1, blocking collectives, steps(): got = lax.all_to_all(spread, CHIPS, 0, 0, tiled=True)  20.1 us
    all_to_all x1, waiting for transfers between devices, steps(): lax.all_to_all(mine.reshape(64, piece, half), CHIPS, 0, 0, tiled=True)  15.1 us
    all_to_all x1, waiting for transfers between devices, steps(): lax.all_to_all(chunks, ('z', 'y', 'core'), 0, 0, tiled=True)  14.1 us
    all_to_all x1, starting transfers between devices, steps(): lax.all_to_all(mine.reshape(64, piece, half), CHIPS, 0, 0, tiled=True)  11.4 us
    pallas_call x1, Pallas kernels, front(): pl.pallas_call(front_kernel, name='front', out_shape=(pltpu.HBM((2, k, n)...  7.8 us
    pallas_call x1, Pallas kernels, backward(): pl.pallas_call(back_kernel, name='back', out_shape=(jax.ShapeDtypeStruct(...  6.89 us
    all_to_all x1, starting transfers between devices, steps(): lax.all_to_all(chunks, ('z', 'y', 'core'), 0, 0, tiled=True)  5.48 us
    pallas_call x1, Pallas kernels, pull_own(): pl.pallas_call(pull_own_kernel, name='pull_own', out_shape=(pltpu.VMEM((2...  3.96 us
  transfers between devices with their start and end apart: 6, of which 4 were waited for; matrix products, arithmetic and copies ran while one was open for 1% of the time, Pallas kernels for 6%

profile of v2, /device:TPU:1, one launch (start us, length us, event | category | flops | bytes accessed | tf_op | source)
XLA Modules:
  0.0 97.8 jit_solution(1741150203226408267)
XLA Ops:
  0.6 0.0 copy-start
  0.6 7.8 %front.1 = (f32[2,512,1024]{2,1,0:T(8,128)}, bf16[2,512,1024]{2,1,0:T(8,128)(2,1)S(1)}, bf16[512,768]{1,0:T(8,128)(2,1)S(1)}, bf16[2,1024,768]{2,1,0:T(8,128)(2,1)S(1)}) custom-call(bf16[2,1024,512]{2,1,0:T(8,128)(2,1)} %sens_hbm.1, bf16[2,1024,1024]{2,1,0:T(8,128)(2,1)} %inv_hbm.3, bf16[2,1024,1536]{2,1,0:T(8,128)(2,1)} %coup_hbm.2), custom_call_target="tpu_custom_call" | custom-call | flops 3758096384 | bytes 13631488 | tf_op jit(solution)/shard_map/front/pallas_call | solution.py:59
  8.5 1.5 %collective-permute-start = (bf16[512,768]{1,0:T(8,128)(2,1)S(1)}, bf16[512,768]{1,0:T(8,128)(2,1)S(1)}, u32[]{:S(2)}, u32[]{:S(2)}) collective-permute-start(bf16[512,768]{1,0:T(8,128)(2,1)S(1)} %get-tuple-element.10), channel_id=1, source_target_pairs={{0,4},{4,0},{1,5},{5,1},{2,6},{6,2},{3,7},{7,3},{8,12},{12,8},{9,1... | collective-permute-start | bytes 2359304 | tf_op jit(solution)/shard_map/ppermute | solution.py:219
  9.9 1.8 %mine.1 = f32[512,768]{1,0:T(8,128)S(1)} custom-call(bf16[2,512,1024]{2,1,0:T(8,128)(2,1)S(1)} %get-tuple-element.8.fwd_half, bf16[2,1024,768]{2,1,0:T(8,128)(2,1)S(1)} %get-tuple-element.9.coup_mine), custom_call_target="tpu_custom_call" | custom-call | flops 1610612736 | bytes 6291456 | tf_op jit(solution)/shard_map/mine/pallas_call | solution.py:89
  11.7 0.1 collective-permute-done
  11.8 1.0 %fusion.1 = bf16[64,8,768]{2,1,0:T(8,128)(2,1)} fusion(f32[512,768]{1,0:T(8,128)S(1)} %mine.1, bf16[512,768]{1,0:T(8,128)(2,1)S(1)} %collective-permute-done), kind=kLoop, calls=%fused_computation.5 | loop fusion | flops 1179648 | bytes 3145728 | tf_op jit(solution)/shard_map/reshape | solution.py:222
  12.9 0.0 copy-start.1
  12.9 11.4 %all-to-all-start = ((bf16[64,8,768]{2,1,0:T(8,128)(2,1)}), bf16[64,8,768]{2,1,0:T(8,128)(2,1)S(1)}, u32[]{:S(2)}, u32[]{:S(2)}) async-start(bf16[64,8,768]{2,1,0:T(8,128)(2,1)} %fusion.1), calls=%async_computation | async-start | bytes 1572864 | tf_op jit(solution)/shard_map/all_to_all | solution.py:222
  24.3 0.0 copy-done.1
  24.3 15.1 %all-to-all-done = bf16[64,8,768]{2,1,0:T(8,128)(2,1)S(1)} async-done(((bf16[64,8,768]{2,1,0:T(8,128)(2,1)}), bf16[64,8,768]{2,1,0:T(8,128)(2,1)S(1)}, u32[]{:S(2)}, u32[]{:S(2)}) %all-to-all-start) | async-done | bytes 786464 | tf_op jit(solution)/shard_map/all_to_all | solution.py:222
  39.5 1.1 %broadcast_in_dim.4 = bf16[16,2,48,384]{3,2,1,0:T(8,128)(2,1)} broadcast(bf16[2,48,384]{2,1,0:T(8,128)(2,1)S(1)} %maximum_select_fusion), dimensions={1,2,3} | broadcast | bytes 1253376 | tf_op jit(solution)/shard_map/broadcast_in_dim | solution.py:215
  40.6 5.5 %all-to-all-start.1 = ((bf16[32,48,384]{2,1,0:T(8,128)(2,1)}), bf16[32,48,384]{2,1,0:T(8,128)(2,1)S(1)}, u32[]{:S(2)}, u32[]{:S(2)}) async-start(bf16[32,48,384]{2,1,0:T(8,128)(2,1)} %bitcast.19), calls=%async_computation.1 | async-start | bytes 2359296 | tf_op jit(solution)/shard_map/all_to_all | solution.py:216
  46.1 0.1 convert_reduce_fusion
  46.2 0.0 copy-done
  46.2 0.3 fusion
  46.5 0.3 collective-permute-start.1
  46.9 2.5 %collective-permute-done.1 = bf16[8,768]{1,0:T(8,128)(2,1)S(1)} collective-permute-done((bf16[8,768]{1,0:T(8,128)(2,1)S(1)}, bf16[8,768]{1,0:T(8,128)(2,1)S(1)}, u32[]{:S(2)}, u32[]{:S(2)}) %collective-permute-start.1) | collective-permute-done | bytes 12320 | tf_op jit(solution)/shard_map/ppermute | solution.py:229
  49.4 1.2 %collective-permute-start.2 = (bf16[16,768]{1,0:T(8,128)(2,1)S(1)}, bf16[16,768]{1,0:T(8,128)(2,1)S(1)}, u32[]{:S(2)}, u32[]{:S(2)}) collective-permute-start(bf16[16,768]{1,0:T(8,128)(2,1)S(1)} %maximum_select_fusion.3), channel_id=1, source_target_pairs={{0,4},{4,0},{1,5},{5,1},{2,6},{6,2},{3,7},{7,3},{8,12},{12,8},{9,1... | collective-permute-start | bytes 73736 | tf_op jit(solution)/shard_map/ppermute | solution.py:231
  50.6 14.1 %all-to-all-done.1 = bf16[32,48,384]{2,1,0:T(8,128)(2,1)S(1)} async-done(((bf16[32,48,384]{2,1,0:T(8,128)(2,1)}), bf16[32,48,384]{2,1,0:T(8,128)(2,1)S(1)}, u32[]{:S(2)}, u32[]{:S(2)}) %all-to-all-start.1) | async-done | bytes 1179680 | tf_op jit(solution)/shard_map/all_to_all | solution.py:216
  64.7 0.0 collective-permute-done.2
  64.7 0.3 convolution_convert_fusion
  65.0 0.1 broadcast_in_dim.5
  65.1 20.1 %all_to_all.15 = bf16[64,16,384]{2,1,0:T(8,128)(2,1)S(1)} all-to-all(bf16[64,16,384]{2,1,0:T(8,128)(2,1)S(1)} %broadcast_in_dim.5), channel_id=1, replica_groups=mesh['z'=4,'y'=4,'core'=2,'xh'=2,'xl'=2] {'z','y','xh','xl'}, dimensions={0} | all-to-all | bytes 1572864 | tf_op jit(solution)/shard_map/all_to_all | solution.py:236
  85.2 1.6 %collective-permute-start.3 = (bf16[64,16,384]{2,1,0:T(8,128)(2,1)S(1)}, bf16[64,16,384]{2,1,0:T(8,128)(2,1)S(1)}, u32[]{:S(2)}, u32[]{:S(2)}) collective-permute-start(bf16[64,16,384]{2,1,0:T(8,128)(2,1)S(1)} %all_to_all.15), channel_id=1, source_target_pairs={{0,4},{4,0},{1,5},{5,1},{2,6},{6,2},{3,7},{7,3},{8,12},{12,8},{9,1... | collective-permute-start | bytes 2359304 | tf_op jit(solution)/shard_map/ppermute | solution.py:238
  86.8 4.0 %pull_own.1 = (f32[2,512,1024]{2,1,0:T(8,128)S(1)}, bf16[2,768,1024]{2,1,0:T(8,128)(2,1)S(1)}) custom-call(bf16[32,2,16,384]{3,2,1,0:T(8,128)(2,1)S(1)} %bitcast.15, bf16[2,1536,1024]{2,1,0:T(8,128)(2,1)} %coup_hbm.3), custom_call_target="tpu_custom_call" | custom-call | flops 1610612736 | bytes 8388608 | tf_op jit(solution)/shard_map/pull_own/pallas_call | solution.py:128
  90.7 0.0 collective-permute-done.3
  90.7 6.9 %back.1 = (bf16[2,1024,512]{2,1,0:T(8,128)(2,1)}, bf16[48,512]{1,0:T(8,128)(2,1)}) custom-call(bf16[32,2,16,384]{3,2,1,0:T(8,128)(2,1)S(1)} %bitcast.16, bf16[32,2,16,384]{3,2,1,0:T(8,128)(2,1)S(1)} %bitcast.17, f32[2,512,1024]{2,1,0:T(8,128)S(1)} %get-tuple-element.11.part, bf16[2,768,1024]{2,1,0:T(8,128)(2,1)S(1)} %get-tuple-element.12.coup, ...), custom_call_target="tpu_custom_call" | custom-call | flops 3758096384 | bytes 20971520 | tf_op jit(solution)/shard_map/back/pallas_call | solution.py:185
  (4 shorter events, 0.1 us)
Async XLA Ops:
  0.6 45.6 %copy-start = (bf16[1536,512]{1,0:T(8,128)(2,1)S(1)}, bf16[1536,512]{1,0:T(8,128)(2,1)}, u32[]{:S(2)}) copy-start(bf16[1536,512]{1,0:T(8,128)(2,1)} %param.10) | copy-start | bytes 4718596
  8.5 3.4 %collective-permute-start = (bf16[512,768]{1,0:T(8,128)(2,1)S(1)}, bf16[512,768]{1,0:T(8,128)(2,1)S(1)}, u32[]{:S(2)}, u32[]{:S(2)}) collective-permute-start(bf16[512,768]{1,0:T(8,128)(2,1)S(1)} %get-tuple-element.10), channel_id=1, source_target_pairs={{0,4},{4,0},{1,5},{5,1},{2,6},{6,2},{3,7},{7,3},{8,12},{12,8},{9,1... | collective-permute-start | bytes 2359304 | tf_op jit(solution)/shard_map/ppermute | solution.py:219
  12.9 11.4 %copy-start.1 = (bf16[48,1536]{1,0:T(8,128)(2,1)S(1)}, bf16[48,1536]{1,0:T(8,128)(2,1)}, u32[]{:S(2)}) copy-start(bf16[48,1536]{1,0:T(8,128)(2,1)} %param.11) | copy-start | bytes 442372
  12.9 26.6 %all-to-all-start = ((bf16[64,8,768]{2,1,0:T(8,128)(2,1)}), bf16[64,8,768]{2,1,0:T(8,128)(2,1)S(1)}, u32[]{:S(2)}, u32[]{:S(2)}) async-start(bf16[64,8,768]{2,1,0:T(8,128)(2,1)} %fusion.1), calls=%async_computation | async-start | bytes 1572864 | tf_op jit(solution)/shard_map/all_to_all | solution.py:222
  40.6 24.1 %all-to-all-start.1 = ((bf16[32,48,384]{2,1,0:T(8,128)(2,1)}), bf16[32,48,384]{2,1,0:T(8,128)(2,1)S(1)}, u32[]{:S(2)}, u32[]{:S(2)}) async-start(bf16[32,48,384]{2,1,0:T(8,128)(2,1)} %bitcast.19), calls=%async_computation.1 | async-start | bytes 2359296 | tf_op jit(solution)/shard_map/all_to_all | solution.py:216
  46.5 2.9 %collective-permute-start.1 = (bf16[8,768]{1,0:T(8,128)(2,1)S(1)}, bf16[8,768]{1,0:T(8,128)(2,1)S(1)}, u32[]{:S(2)}, u32[]{:S(2)}) collective-permute-start(bf16[8,768]{1,0:T(8,128)(2,1)S(1)} %fusion), channel_id=1, source_target_pairs={{0,1},{1,0},{2,3},{3,2},{4,5},{5,4},{6,7},{7,6},{8,9},{9,8},{10,11... | collective-permute-start | bytes 36872 | tf_op jit(solution)/shard_map/ppermute | solution.py:229
  49.4 15.3 %collective-permute-start.2 = (bf16[16,768]{1,0:T(8,128)(2,1)S(1)}, bf16[16,768]{1,0:T(8,128)(2,1)S(1)}, u32[]{:S(2)}, u32[]{:S(2)}) collective-permute-start(bf16[16,768]{1,0:T(8,128)(2,1)S(1)} %maximum_select_fusion.3), channel_id=1, source_target_pairs={{0,4},{4,0},{1,5},{5,1},{2,6},{6,2},{3,7},{7,3},{8,12},{12,8},{9,1... | collective-permute-start | bytes 73736 | tf_op jit(solution)/shard_map/ppermute | solution.py:231
  85.2 5.5 %collective-permute-start.3 = (bf16[64,16,384]{2,1,0:T(8,128)(2,1)S(1)}, bf16[64,16,384]{2,1,0:T(8,128)(2,1)S(1)}, u32[]{:S(2)}, u32[]{:S(2)}) collective-permute-start(bf16[64,16,384]{2,1,0:T(8,128)(2,1)S(1)} %all_to_all.15), channel_id=1, source_target_pairs={{0,4},{4,0},{1,5},{5,1},{2,6},{6,2},{3,7},{7,3},{8,12},{12,8},{9,1... | collective-permute-start | bytes 2359304 | tf_op jit(solution)/shard_map/ppermute | solution.py:238

commit v3 on v1

v3 whole, which is shorter than its diff:
```python
import jax
import jax.numpy as jnp
from jax import lax
from jax.experimental import pallas as pl
from jax.experimental.pallas import tpu as pltpu
from jax.sharding import Mesh, PartitionSpec as P

F32 = jnp.float32
BF16 = jnp.bfloat16
CHIPS = ("z", "y", "xh", "xl")
SWAP = [(0, 1), (1, 0)]
NEAR = [(0, 1), (1, 0), (2, 3), (3, 2)]
FAR = [(0, 3), (3, 0), (1, 2), (2, 1)]
ORDER = (0, 2, 3, 1)
HBM = pl.BlockSpec(memory_space=pltpu.HBM)
VMEM = pl.BlockSpec(memory_space=pltpu.VMEM)


def call(kernel, outs, ins, operands, scratch=(), mib=16, flops=0, mbytes=1, alias={}):
    return pl.pallas_call(
        kernel,
        out_shape=outs,
        in_specs=ins,
        out_specs=[VMEM if str(o.memory_space) == "vmem" else HBM for o in outs],
        scratch_shapes=list(scratch),
        input_output_aliases=alias,
        compiler_params=pltpu.CompilerParams(vmem_limit_bytes=mib << 20),
        cost_estimate=pl.CostEstimate(flops=flops, bytes_accessed=mbytes << 20, transcendentals=0),
    )(*[pltpu.with_memory_space_constraint(x, s.memory_space) for x, s in zip(operands, ins)])


def dot(a, b):
    return jnp.dot(a, b, preferred_element_type=F32)


def lanes(index, size):
    return pl.ds(pl.multiple_of(index * size, 128), size)


def forward_kernel(sens_hbm, inv_hbm, coup_hbm, fwd_hbm, fwd, away, coup0, coup1, inv, sens, turned, sems):
    half = away.shape[0]
    core = lax.axis_index("core")
    loads = []
    for b in range(2):
        loads.append(pltpu.make_async_copy(sens_hbm.at[b], sens.at[b], sems.at[2 * b]))
        loads.append(pltpu.make_async_copy(inv_hbm.at[b], inv.at[b], sems.at[2 * b + 1]))
    coup = (coup0, coup1)
    loads += [pltpu.make_async_copy(coup_hbm.at[b], coup[b], sems.at[4 + b]) for b in range(2)]
    stores = [pltpu.make_async_copy(fwd.at[b], fwd_hbm.at[b], sems.at[6 + b]) for b in range(2)]
    for load in loads:
        load.start()
    for b in range(2):
        loads[2 * b].wait()
        turned[b] = sens[b].T
        loads[2 * b + 1].wait()
        fwd[b] = dot(turned[b], inv[b]).astype(BF16)
        stores[b].start()
    loads[4].wait()
    total = dot(fwd[0, lanes(1 - core, half), :], coup0[...])
    loads[5].wait()
    away[...] = (total + dot(fwd[1, lanes(1 - core, half), :], coup1[...])).astype(BF16)
    for store in stores:
        store.wait()


def mine_kernel(fwd, coup0, coup1, out):
    half = out.shape[0]
    core = lax.axis_index("core")
    out[...] = dot(fwd[0, lanes(core, half), :], coup0[...]) + dot(fwd[1, lanes(core, half), :], coup1[...])


def order_kernel(ring0, ring1, ring2, ring3, out):
    yed = lax.axis_index("y")
    for step, ring in enumerate((ring0, ring1, ring2, ring3)):
        out[lax.rem(yed + 4 - step, 4)] = ring[...]


def join_kernel(mine, came, out_hbm, out, sems):
    quarter = out.shape[2]
    copies = []
    for z in range(4):
        span = slice(z * quarter, (z + 1) * quarter)
        value = (mine[:, span] + came[:, span].astype(F32)).astype(BF16)
        out[z * 16:(z + 1) * 16] = value.reshape(16, -1, quarter)
        copies.append(pltpu.make_async_copy(out.at[z * 16:(z + 1) * 16], out_hbm.at[z * 16:(z + 1) * 16], sems.at[z]))
        copies[-1].start()
    for copy in copies:
        copy.wait()


def unroll(got, lhs):
    quarter = got.shape[2]
    for z in range(4):
        lhs[:, ORDER[z] * quarter:(ORDER[z] + 1) * quarter] = got[z * 16:(z + 1) * 16].reshape(-1, quarter)


def finish(b, pulled, inv, fwd, adjoint, adjoint_hbm, sems, columns):
    stores = []
    step = inv.shape[2] // 4
    for i in range(4):
        span = slice(i * step, (i + 1) * step)
        value = fwd[b, :, span].astype(F32) - dot(pulled[b], inv[b, :, span])
        adjoint[b, span, :] = value.astype(BF16).T
        stores.append(pltpu.make_async_copy(adjoint.at[b, span, :], adjoint_hbm.at[b, span, columns], sems.at[4 * b + i]))
        stores[-1].start()
    return stores


def own_kernel(got, coup_hbm, inv_hbm, fwd_hbm, adjoint_hbm, coup, inv, fwd, adjoint, lhs, pulled, sems, out_sems):
    half = lhs.shape[0]
    core = lax.axis_index("core")
    third = coup.shape[1] // 3
    loads = []
    for b in range(2):
        for i in range(3):
            span = slice(i * third, (i + 1) * third)
            loads.append(pltpu.make_async_copy(coup_hbm.at[b, span, :], coup.at[b, span, :], sems.at[5 * b + i]))
        loads.append(pltpu.make_async_copy(inv_hbm.at[b], inv.at[b], sems.at[5 * b + 3]))
        loads.append(pltpu.make_async_copy(fwd_hbm.at[b, lanes(core, half), :], fwd.at[b], sems.at[5 * b + 4]))
    for load in loads:
        load.start()
    unroll(got, lhs)
    stores = []
    for b in range(2):
        total = None
        for i in range(3):
            span = slice(i * third, (i + 1) * third)
            loads[5 * b + i].wait()
            value = dot(lhs[:, span], coup[b, span, :])
            total = value if total is None else total + value
        pulled[b] = total.astype(BF16)
        loads[5 * b + 3].wait()
        loads[5 * b + 4].wait()
        stores += finish(b, pulled, inv, fwd, adjoint, adjoint_hbm, out_sems, lanes(core, half))
    for store in stores:
        store.wait()


def other_kernel(own, other, coup, inv, fwd_hbm, _, adjoint_hbm, border_hbm, fwd, adjoint, border, lhs, pulled, sems, out_sems):
    half, quarter = lhs.shape[0], own.shape[2]
    core = lax.axis_index("core")
    zed = lax.axis_index("z")
    loads = [pltpu.make_async_copy(fwd_hbm.at[b, lanes(1 - core, half), :], fwd.at[b], sems.at[b]) for b in range(2)]
    for load in loads:
        load.start()
    unroll(other, lhs)
    stores = []
    for b in range(2):
        pulled[b] = dot(lhs[...], coup[b]).astype(BF16)
        loads[b].wait()
        stores += finish(b, pulled, inv, fwd, adjoint, adjoint_hbm, out_sems, lanes(1 - core, half))
        if b == 0:
            rows = border.shape[0]
            first = (lax.axis_index("y") * 2 + core) * rows
            spot = first + lax.broadcasted_iota(jnp.int32, (rows, quarter), 0)
            pick = (lax.broadcasted_iota(jnp.int32, (rows, quarter), 1) == spot).astype(BF16)
            source = jnp.where(zed == 0, 0, jnp.where(zed == 1, 3, zed - 1))
            for ref, side in ((own, core), (other, 1 - core)):
                chosen = ref[pl.ds(source * 16, 16)].reshape(-1, quarter)
                picked = lax.dot_general(pick, chosen, (((1,), (1,)), ((), ())), preferred_element_type=F32)
                border[:, lanes(side, half)] = picked.astype(BF16)
            stores.append(pltpu.make_async_copy(border, border_hbm, sems.at[2]))
            stores[-1].start()
    for store in stores:
        store.wait()


def steps(block_inverse, coupling_in, coupling_out, sensitivities, border_rhs, border_inverse):
    core = lax.axis_index("core")
    zed = lax.axis_index("z")
    rows, link = border_inverse.shape
    n, cols = sensitivities.shape[1:]
    half, quarter = cols // 2, link // 4
    piece = cols // 32
    sem = pltpu.SemaphoreType.DMA

    ring = [border_inverse]
    for step in (1, 2, 3):
        ring.append(lax.ppermute(border_inverse, "y", [(i, (i + step) % 4) for i in range(4)]))
    ring, = call(order_kernel, (pltpu.VMEM((4, rows, link), BF16),), [VMEM] * 4, ring, (), 2)
    other = lax.ppermute(ring, "core", SWAP)
    plane = jnp.where(core == 0, jnp.stack([ring, other], 1), jnp.stack([other, ring], 1)).reshape(quarter, link)

    fwd, fwd_near, away, coup0, coup1 = call(
        forward_kernel,
        (pltpu.HBM((2, cols, n), BF16), pltpu.VMEM((2, cols, n), BF16), pltpu.VMEM((half, link), BF16)) + (pltpu.VMEM((n, link), BF16),) * 2,
        [HBM] * 3, (sensitivities, block_inverse, coupling_in),
        [pltpu.VMEM((2, n, n), BF16), pltpu.VMEM((2, n, cols), BF16), pltpu.VMEM((2, cols, n), BF16), sem((8,))],
        24, 4 * n * cols * (n + link // 2), 17)
    came = lax.ppermute(away, "core", SWAP)
    mine, = call(mine_kernel, (pltpu.VMEM((half, link), F32),), [VMEM] * 3, (fwd_near, coup0, coup1), (), 8, 4 * n * half * link, 9)
    terms, = call(
        join_kernel, (pltpu.HBM((64, piece, quarter), BF16),), [VMEM] * 2, (mine, came),
        [pltpu.VMEM((64, piece, quarter), BF16), sem((4,))], 4, 0, 3)
    parts = lax.all_to_all(terms, CHIPS, 0, 0, tiled=True)
    total = jnp.sum(parts.astype(F32), axis=0)

    start = core * half + lax.axis_index(("y", "xh", "xl")) * piece
    pick = (lax.broadcasted_iota(jnp.int32, (piece, cols), 1) == start + lax.broadcasted_iota(jnp.int32, (piece, cols), 0)).astype(BF16)
    rhs_part = lax.dynamic_slice_in_dim(border_rhs, zed * quarter, quarter, 0)
    rhs = lax.dot_general(pick, rhs_part, (((1,), (1,)), ((), ())), preferred_element_type=F32)
    residual = (rhs - total).astype(BF16)
    share = dot(residual, plane)
    inner = ((zed == 1) | (zed == 2)).astype(jnp.int32)
    outer = zed // 2
    came = lax.ppermute(lax.dynamic_slice_in_dim(share, (1 - inner) * 2 * quarter, 2 * quarter, 1), "z", NEAR)
    share = lax.dynamic_slice_in_dim(share, inner * 2 * quarter, 2 * quarter, 1) + came
    came = lax.ppermute(lax.dynamic_slice_in_dim(share, (1 - outer) * quarter, quarter, 1), "z", FAR)
    solved = (lax.dynamic_slice_in_dim(share, outer * quarter, quarter, 1) + came).astype(BF16)

    spread = jnp.broadcast_to(solved[None], (64,) + solved.shape)
    own = lax.all_to_all(spread, CHIPS, 0, 0, tiled=True)
    other = lax.ppermute(own, "core", SWAP)

    buffers = [pltpu.VMEM((2, half, n), BF16), pltpu.VMEM((2, n, half), BF16)]
    more = [pltpu.VMEM((half, link), BF16), pltpu.VMEM((2, half, n), BF16)]
    adjoint, coup, inv = call(
        own_kernel, (pltpu.HBM((2, n, cols), BF16), pltpu.VMEM((2, link, n), BF16), pltpu.VMEM((2, n, n), BF16)),
        [VMEM] + [HBM] * 3, (own, coupling_out, block_inverse, fwd), buffers + more + [sem((10,)), sem((8,))],
        12, 4 * half * n * (n + link), 14)
    return call(
        other_kernel, (pltpu.HBM((2, n, cols), BF16), pltpu.HBM((rows, cols), BF16)), [VMEM] * 4 + [HBM] * 2,
        (own, other, coup, inv, fwd, adjoint), buffers + [pltpu.VMEM((rows, cols), BF16)] + more + [sem((3,)), sem((8,))],
        12, 4 * half * n * (n + link), 14, {5: 0})


def body(*args):
    return tuple(steps(*args))


def solution(mesh):
    mesh = Mesh(mesh.devices.reshape(4, 4, 2, 2, 2), ("z", "y", "core", "xh", "xl"))
    every = ("z", "y", "core", "xh", "xl")
    blocks = P(every, None, None)
    lines = P(("z", "y", "core"), None)
    return jax.shard_map(
        body, mesh=mesh, in_specs=(blocks, blocks, blocks, blocks, P(), lines), out_specs=(blocks, lines), check_vma=False
    )
```

time: 118 us -> 90.8 us (0.77)
  matrix products: 28.3 us -> 1.25 us
  Pallas kernels: 0 us -> 20.2 us
  local copies, waits for them, and re-layouts: 9.58 us -> 0.18 us
  waiting for transfers between devices: 33.4 us -> 26 us
  blocking collectives: 20.1 us -> 16.3 us
  starting transfers between devices: 21.5 us -> 24.6 us
  other arithmetic: 3.98 us -> 0.97 us
    dot_general x7 -> x1, matrix products: 28.3 us -> 1.25 us  [dot(): return jnp.dot(a, b, preferred_element_type=F32)]
    pallas_call x0 -> x6, Pallas kernels: none -> 20.2 us  [call(): pl.pallas_call(kernel, out_shape=outs, in_specs=ins, out_specs=[VMEM if s...]
    all_to_all x2 -> x1, waiting for transfers between devices: 26.8 us -> 15.2 us  [steps(): parts = lax.all_to_all(terms, CHIPS, 0, 0, tiled=True)]
    ppermute x4 -> x8, starting transfers between devices: 4.8 us -> 13.9 us  [the longest x3 5.7 us: steps(): lax.ppermute(border_inverse, 'y', [(i, (i + step) % 4) for i in range(4)])]
    unnamed x14 -> x4, local copies, waits for them, and re-layouts: 7.37 us -> 0.01 us
    all_to_all x2 -> x1, starting transfers between devices: 16.7 us -> 10.6 us  [steps(): parts = lax.all_to_all(terms, CHIPS, 0, 0, tiled=True)]
    ppermute x4 -> x8, waiting for transfers between devices: 6.63 us -> 10.8 us  [the longest x3 4.72 us: steps(): lax.ppermute(border_inverse, 'y', [(i, (i + step) % 4) for i in range(4)])]
    all_to_all x1, blocking collectives: 20.1 us -> 16.3 us  [steps(): own = lax.all_to_all(spread, CHIPS, 0, 0, tiled=True)]
  transfers between devices with their start and end apart: 6 -> 9, of which waited for: 5 -> 6; matrix products, arithmetic and copies ran while one was open for 3% -> 0% of each run, Pallas kernels for 0% -> 10%
where the time goes in v3:
time: 90.8 us; the launch traced here: 90.5 us
  waiting for transfers between devices  26 us (29%)
  starting transfers between devices  24.6 us (27%)
  Pallas kernels  20.2 us (22%)
  blocking collectives  16.3 us (18%)
  matrix products  1.25 us (1%)
  other arithmetic  0.97 us (1%)
  between operations  0.97 us (1%)
    pallas_call x6, Pallas kernels, call(): pl.pallas_call(kernel, out_shape=outs, in_specs=ins, out_specs=[VMEM if s...  20.2 us
    all_to_all x1, blocking collectives, steps(): own = lax.all_to_all(spread, CHIPS, 0, 0, tiled=True)  16.3 us
    all_to_all x1, waiting for transfers between devices, steps(): parts = lax.all_to_all(terms, CHIPS, 0, 0, tiled=True)  15.2 us
    all_to_all x1, starting transfers between devices, steps(): parts = lax.all_to_all(terms, CHIPS, 0, 0, tiled=True)  10.6 us
    ppermute x3, starting transfers between devices, steps(): lax.ppermute(border_inverse, 'y', [(i, (i + step) % 4) for i in range(4)])  5.7 us
    ppermute x1, starting transfers between devices, steps(): other = lax.ppermute(own, 'core', SWAP)  4.89 us
    ppermute x3, waiting for transfers between devices, steps(): lax.ppermute(border_inverse, 'y', [(i, (i + step) % 4) for i in range(4)])  4.72 us
    ppermute x1, waiting for transfers between devices, steps(): lax.ppermute(lax.dynamic_slice_in_dim(share, (1 - outer) * quarter, quart...  3.19 us
  transfers between devices with their start and end apart: 9, of which 6 were waited for; matrix products, arithmetic and copies ran while one was open for 0% of the time, Pallas kernels for 10%

profile of v3, /device:TPU:1, one launch (start us, length us, event | category | flops | bytes accessed | tf_op | source)
XLA Modules:
  0.0 90.5 jit_solution(15087326110481015281)
XLA Ops:
  0.6 0.0 copy-start
  0.6 0.0 copy-start.1
  0.7 7.0 %shard_map.77 = (bf16[2,512,1024]{2,1,0:T(8,128)(2,1)}, bf16[2,512,1024]{2,1,0:T(8,128)(2,1)S(1)}, bf16[256,1536]{1,0:T(8,128)(2,1)S(1)}, bf16[1024,1536]{1,0:T(8,128)(2,1)S(1)}, bf16[1024,1536]{1,0:T(8,128)(2,1)S(1)}) custom-call(bf16[2,1024,512]{2,1,0:T(8,128)(2,1)} %sens_hbm.1, bf16[2,1024,1024]{2,1,0:T(8,128)(2,1)} %inv_hbm.3, ...), custom_call_target="tpu_custom_call" | custom-call | flops 3758096384 | bytes 17825792 | tf_op jit(solution)/shard_map/pallas_call | solution.py:20
  7.7 1.5 %collective-permute-start = (bf16[256,1536]{1,0:T(8,128)(2,1)S(1)}, bf16[256,1536]{1,0:T(8,128)(2,1)S(1)}, u32[]{:S(2)}, u32[]{:S(2)}) collective-permute-start(bf16[256,1536]{1,0:T(8,128)(2,1)S(1)} %get-tuple-element.13), channel_id=1, source_target_pairs={{0,4},{4,0},{1,5},{5,1},{2,6},{6,2},{3,7},{7,3},{8,12},{12,8},{9,1... | collective-permute-start | bytes 2359304 | tf_op jit(solution)/shard_map/ppermute | solution.py:190
  9.2 0.0 copy-done.1
  9.2 3.0 %collective-permute-start.2 = (bf16[48,1536]{1,0:T(8,128)(2,1)S(1)}, bf16[48,1536]{1,0:T(8,128)(2,1)S(1)}, u32[]{:S(2)}, u32[]{:S(2)}) collective-permute-start(bf16[48,1536]{1,0:T(8,128)(2,1)S(1)} %copy-done.1), channel_id=1, source_target_pairs={{0,16},{8,24},{16,0},{24,8},{1,17},{9,25},{17,1},{25,9},{2,18},{10... | collective-permute-start | bytes 442376 | tf_op jit(solution)/shard_map/ppermute | solution.py:179
  12.2 0.4 collective-permute-start.1
  12.6 2.3 %collective-permute-start.3 = (bf16[48,1536]{1,0:T(8,128)(2,1)S(1)}, bf16[48,1536]{1,0:T(8,128)(2,1)S(1)}, u32[]{:S(2)}, u32[]{:S(2)}) collective-permute-start(bf16[48,1536]{1,0:T(8,128)(2,1)S(1)} %copy-done.1), channel_id=1, source_target_pairs={{0,24},{8,0},{16,8},{24,16},{1,25},{9,1},{17,9},{25,17},{2,26},{10... | collective-permute-start | bytes 442376 | tf_op jit(solution)/shard_map/ppermute | solution.py:179
  14.9 1.2 %collective-permute-done.2.ring2 = bf16[48,1536]{1,0:T(8,128)(2,1)S(1)} collective-permute-done((bf16[48,1536]{1,0:T(8,128)(2,1)S(1)}, bf16[48,1536]{1,0:T(8,128)(2,1)S(1)}, u32[]{:S(2)}, u32[]{:S(2)}) %collective-permute-start.2) | collective-permute-done | bytes 147488 | tf_op jit(solution)/shard_map/ppermute | solution.py:179
  16.1 3.2 %collective-permute-done.1.ring1 = bf16[48,1536]{1,0:T(8,128)(2,1)S(1)} collective-permute-done((bf16[48,1536]{1,0:T(8,128)(2,1)S(1)}, bf16[48,1536]{1,0:T(8,128)(2,1)S(1)}, u32[]{:S(2)}, u32[]{:S(2)}) %collective-permute-start.1) | collective-permute-done | bytes 147488 | tf_op jit(solution)/shard_map/ppermute | solution.py:179
  19.3 0.2 collective-permute-done.3.ring3
  19.6 0.1 shard_map.80
  19.6 1.0 %collective-permute-start.4 = (bf16[4,48,1536]{2,1,0:T(8,128)(2,1)S(1)}, bf16[4,48,1536]{2,1,0:T(8,128)(2,1)S(1)}, u32[]{:S(2)}, u32[]{:S(2)}) collective-permute-start(bf16[4,48,1536]{2,1,0:T(8,128)(2,1)S(1)} %shard_map.80), channel_id=1, source_target_pairs={{0,4},{4,0},{1,5},{5,1},{2,6},{6,2},{3,7},{7,3},{8,12},{12,8},{9,1... | collective-permute-start | bytes 1769480 | tf_op jit(solution)/shard_map/ppermute | solution.py:181
  20.7 1.8 %shard_map.78.mine = f32[256,1536]{1,0:T(8,128)S(1)} custom-call(bf16[2,512,1024]{2,1,0:T(8,128)(2,1)S(1)} %get-tuple-element.10.fwd, bf16[1024,1536]{1,0:T(8,128)(2,1)S(1)} %get-tuple-element.11.coup0, bf16[1024,1536]{1,0:T(8,128)(2,1)S(1)} %get-tuple-element.12.coup1), custom_call_target="tpu_custom_call" | custom-call | flops 1610612736 | bytes 9437184 | tf_op jit(solution)/shard_map/pallas_call | solution.py:20
  22.5 0.0 collective-permute-done.came
  22.5 0.9 %shard_map.79 = bf16[64,16,384]{2,1,0:T(8,128)(2,1)} custom-call(f32[256,1536]{1,0:T(8,128)S(1)} %shard_map.78.mine, bf16[256,1536]{1,0:T(8,128)(2,1)S(1)} %collective-permute-done.came), custom_call_target="tpu_custom_call" | custom-call | bytes 3145728 | tf_op jit(solution)/shard_map/pallas_call | solution.py:20
  23.4 10.6 %all-to-all-start = ((bf16[64,16,384]{2,1,0:T(8,128)(2,1)}), bf16[64,16,384]{2,1,0:T(8,128)(2,1)S(1)}, u32[]{:S(2)}, u32[]{:S(2)}) async-start(bf16[64,16,384]{2,1,0:T(8,128)(2,1)} %shard_map.79), calls=%async_computation | async-start | bytes 1572864 | tf_op jit(solution)/shard_map/all_to_all | solution.py:195
  34.1 0.0 collective-permute-done.4
  34.1 0.2 maximum_select_fusion
  34.3 0.1 copy.9
  34.4 15.2 %all-to-all-done = bf16[64,16,384]{2,1,0:T(8,128)(2,1)S(1)} async-done(((bf16[64,16,384]{2,1,0:T(8,128)(2,1)}), bf16[64,16,384]{2,1,0:T(8,128)(2,1)S(1)}, u32[]{:S(2)}, u32[]{:S(2)}) %all-to-all-start) | async-done | bytes 786464 | tf_op jit(solution)/shard_map/all_to_all | solution.py:195
  49.6 0.7 convert_reduce_fusion
  50.4 0.0 copy-done
  50.4 1.2 %fusion.1 = f32[16,1536]{1,0:T(8,128)S(1)} fusion(bf16[384,1536]{1,0:T(8,128)(2,1)S(1)} %bitcast.5, f32[16,384]{1,0:T(8,128)} %convert_reduce_fusion, bf16[1536,512]{1,0:T(8,128)(2,1)S(1)} %copy-done, s32[]{:T(128)S(6)} %select_n.32, s32[16]{0:T(128)S(1)} %iota_add_fusion), kind=kOutput, calls=%fused_computation.4 | convolution fusion | flops 25186304 | bytes 1696260 | tf_op jit(solution)/shard_map/dot_general | solution.py:33
  51.6 0.1 collective-permute-start.5
  51.7 2.9 %collective-permute-done.5 = f32[16,768]{1,0:T(8,128)S(1)} collective-permute-done((f32[16,768]{1,0:T(8,128)S(1)}, f32[16,768]{1,0:T(8,128)S(1)}, u32[]{:S(2)}, u32[]{:S(2)}) %collective-permute-start.5) | collective-permute-done | bytes 49184 | tf_op jit(solution)/shard_map/ppermute | solution.py:206
  54.7 0.8 collective-permute-start.6
  55.4 3.2 %collective-permute-done.6 = f32[16,384]{1,0:T(8,128)S(1)} collective-permute-done((f32[16,384]{1,0:T(8,128)S(1)}, f32[16,384]{1,0:T(8,128)S(1)}, u32[]{:S(2)}, u32[]{:S(2)}) %collective-permute-start.6) | collective-permute-done | bytes 24608 | tf_op jit(solution)/shard_map/ppermute | solution.py:208
  58.6 0.1 broadcast_in_dim.2
  58.7 16.3 %all_to_all.10.got.own = bf16[64,16,384]{2,1,0:T(8,128)(2,1)S(1)} all-to-all(bf16[64,16,384]{2,1,0:T(8,128)(2,1)S(1)} %broadcast_in_dim.2), channel_id=1, replica_groups=mesh['z'=4,'y'=4,'core'=2,'xh'=2,'xl'=2] {'z','y','xh','xl'}, dimensions={0} | all-to-all | bytes 1572864 | tf_op jit(solution)/shard_map/all_to_all | solution.py:212
  75.1 4.9 %collective-permute-start.7 = (bf16[64,16,384]{2,1,0:T(8,128)(2,1)S(1)}, bf16[64,16,384]{2,1,0:T(8,128)(2,1)S(1)}, u32[]{:S(2)}, u32[]{:S(2)}) collective-permute-start(bf16[64,16,384]{2,1,0:T(8,128)(2,1)S(1)} %all_to_all.10.got.own), channel_id=1, source_target_pairs={{0,4},{4,0},{1,5},{5,1},{2,6},{6,2},{3,7},{7,3},{8,12},{12,8},{9,1... | collective-permute-start | bytes 2359304 | tf_op jit(solution)/shard_map/ppermute | solution.py:213
  79.9 6.1 %shard_map.81 = (bf16[2,1024,512]{2,1,0:T(8,128)(2,1)}, bf16[2,1536,1024]{2,1,0:T(8,128)(2,1)S(1)}, bf16[2,1024,1024]{2,1,0:T(8,128)(2,1)S(1)}) custom-call(bf16[64,16,384]{2,1,0:T(8,128)(2,1)S(1)} %all_to_all.10.got.own, bf16[2,1536,1024]{2,1,0:T(8,128)(2,1)} %coup_hbm.3, bf16[2,1024,1024]{2,1,0:T(8,128)(2,1)} %inv_hbm.3, ...), custom_call_target="tpu_custom_call" | custom-call | flops 2684354560 | bytes 14680064 | tf_op jit(solution)/shard_map/pallas_call | solution.py:20
  86.1 0.0 collective-permute-done.7.other
  86.1 4.3 %shard_map.82 = (bf16[2,1024,512]{2,1,0:T(8,128)(2,1)}, bf16[48,512]{1,0:T(8,128)(2,1)}) custom-call(bf16[64,16,384]{2,1,0:T(8,128)(2,1)S(1)} %all_to_all.10.got.own, bf16[64,16,384]{2,1,0:T(8,128)(2,1)S(1)} %collective-permute-done.7.other, bf16[2,1536,1024]{2,1,0:T(8,128)(2,1)S(1)} %get-tuple-element.15.coup, ...), custom_call_target="tpu_custom_call", output_to_operand_aliasing={{0}: (5, {})} | custom-call | flops 2684354560 | bytes 14680064 | tf_op jit(solution)/shard_map/pallas_call | solution.py:20
  (5 shorter events, 0.0 us)
Async XLA Ops:
  0.6 49.7 %copy-start = (bf16[1536,512]{1,0:T(8,128)(2,1)S(1)}, bf16[1536,512]{1,0:T(8,128)(2,1)}, u32[]{:S(2)}) copy-start(bf16[1536,512]{1,0:T(8,128)(2,1)} %param.10) | copy-start | bytes 4718596
  0.6 8.5 %copy-start.1 = (bf16[48,1536]{1,0:T(8,128)(2,1)S(1)}, bf16[48,1536]{1,0:T(8,128)(2,1)}, u32[]{:S(2)}) copy-start(bf16[48,1536]{1,0:T(8,128)(2,1)} %ring0.1) | copy-start | bytes 442372
  7.7 14.8 %collective-permute-start = (bf16[256,1536]{1,0:T(8,128)(2,1)S(1)}, bf16[256,1536]{1,0:T(8,128)(2,1)S(1)}, u32[]{:S(2)}, u32[]{:S(2)}) collective-permute-start(bf16[256,1536]{1,0:T(8,128)(2,1)S(1)} %get-tuple-element.13), channel_id=1, source_target_pairs={{0,4},{4,0},{1,5},{5,1},{2,6},{6,2},{3,7},{7,3},{8,12},{12,8},{9,1... | collective-permute-start | bytes 2359304 | tf_op jit(solution)/shard_map/ppermute | solution.py:190
  9.2 6.9 %collective-permute-start.2 = (bf16[48,1536]{1,0:T(8,128)(2,1)S(1)}, bf16[48,1536]{1,0:T(8,128)(2,1)S(1)}, u32[]{:S(2)}, u32[]{:S(2)}) collective-permute-start(bf16[48,1536]{1,0:T(8,128)(2,1)S(1)} %copy-done.1), channel_id=1, source_target_pairs={{0,16},{8,24},{16,0},{24,8},{1,17},{9,25},{17,1},{25,9},{2,18},{10... | collective-permute-start | bytes 442376 | tf_op jit(solution)/shard_map/ppermute | solution.py:179
  12.2 7.2 %collective-permute-start.1 = (bf16[48,1536]{1,0:T(8,128)(2,1)S(1)}, bf16[48,1536]{1,0:T(8,128)(2,1)S(1)}, u32[]{:S(2)}, u32[]{:S(2)}) collective-permute-start(bf16[48,1536]{1,0:T(8,128)(2,1)S(1)} %copy-done.1), channel_id=1, source_target_pairs={{0,8},{8,16},{16,24},{24,0},{1,9},{9,17},{17,25},{25,1},{2,10},{10... | collective-permute-start | bytes 442376 | tf_op jit(solution)/shard_map/ppermute | solution.py:179
  12.6 7.0 %collective-permute-start.3 = (bf16[48,1536]{1,0:T(8,128)(2,1)S(1)}, bf16[48,1536]{1,0:T(8,128)(2,1)S(1)}, u32[]{:S(2)}, u32[]{:S(2)}) collective-permute-start(bf16[48,1536]{1,0:T(8,128)(2,1)S(1)} %copy-done.1), channel_id=1, source_target_pairs={{0,24},{8,0},{16,8},{24,16},{1,25},{9,1},{17,9},{25,17},{2,26},{10... | collective-permute-start | bytes 442376 | tf_op jit(solution)/shard_map/ppermute | solution.py:179
  19.6 14.5 %collective-permute-start.4 = (bf16[4,48,1536]{2,1,0:T(8,128)(2,1)S(1)}, bf16[4,48,1536]{2,1,0:T(8,128)(2,1)S(1)}, u32[]{:S(2)}, u32[]{:S(2)}) collective-permute-start(bf16[4,48,1536]{2,1,0:T(8,128)(2,1)S(1)} %shard_map.80), channel_id=1, source_target_pairs={{0,4},{4,0},{1,5},{5,1},{2,6},{6,2},{3,7},{7,3},{8,12},{12,8},{9,1... | collective-permute-start | bytes 1769480 | tf_op jit(solution)/shard_map/ppermute | solution.py:181
  23.4 26.2 %all-to-all-start = ((bf16[64,16,384]{2,1,0:T(8,128)(2,1)}), bf16[64,16,384]{2,1,0:T(8,128)(2,1)S(1)}, u32[]{:S(2)}, u32[]{:S(2)}) async-start(bf16[64,16,384]{2,1,0:T(8,128)(2,1)} %shard_map.79), calls=%async_computation | async-start | bytes 1572864 | tf_op jit(solution)/shard_map/all_to_all | solution.py:195
  51.6 3.0 %collective-permute-start.5 = (f32[16,768]{1,0:T(8,128)S(1)}, f32[16,768]{1,0:T(8,128)S(1)}, u32[]{:S(2)}, u32[]{:S(2)}) collective-permute-start(f32[16,768]{1,0:T(8,128)S(1)} %constant_dynamic-slice_fusion.1), channel_id=1, source_target_pairs={{0,32},{32,0},{64,96},{96,64},{1,33},{33,1},{65,97},{97,65},{2,34}... | collective-permute-start | bytes 147464 | tf_op jit(solution)/shard_map/ppermute | solution.py:206
  54.7 4.0 %collective-permute-start.6 = (f32[16,384]{1,0:T(8,128)S(1)}, f32[16,384]{1,0:T(8,128)S(1)}, u32[]{:S(2)}, u32[]{:S(2)}) collective-permute-start(f32[16,384]{1,0:T(8,128)S(1)} %constant_dynamic-slice_fusion), channel_id=1, source_target_pairs={{0,96},{96,0},{32,64},{64,32},{1,97},{97,1},{33,65},{65,33},{2,98}... | collective-permute-start | bytes 73736 | tf_op jit(solution)/shard_map/ppermute | solution.py:208
  75.1 11.1 %collective-permute-start.7 = (bf16[64,16,384]{2,1,0:T(8,128)(2,1)S(1)}, bf16[64,16,384]{2,1,0:T(8,128)(2,1)S(1)}, u32[]{:S(2)}, u32[]{:S(2)}) collective-permute-start(bf16[64,16,384]{2,1,0:T(8,128)(2,1)S(1)} %all_to_all.10.got.own), channel_id=1, source_target_pairs={{0,4},{4,0},{1,5},{5,1},{2,6},{6,2},{3,7},{7,3},{8,12},{12,8},{9,1... | collective-permute-start | bytes 2359304 | tf_op jit(solution)/shard_map/ppermute | solution.py:213

commit v4 on v3

v4 whole, which is shorter than its diff:
```python
import jax
import jax.numpy as jnp
from jax import lax
from jax.experimental import pallas as pl
from jax.experimental.pallas import tpu as pltpu
from jax.sharding import Mesh, PartitionSpec as P

F32 = jnp.float32
BF16 = jnp.bfloat16
CHIPS = ("z", "y", "xh", "xl")
SWAP = [(0, 1), (1, 0)]
NEAR = [(0, 1), (1, 0), (2, 3), (3, 2)]
FAR = [(0, 3), (3, 0), (1, 2), (2, 1)]
ORDER = (0, 2, 3, 1)
HBM = pl.BlockSpec(memory_space=pltpu.HBM)
VMEM = pl.BlockSpec(memory_space=pltpu.VMEM)


def call(kernel, outs, ins, operands, scratch=(), mib=16, flops=0, mbytes=1, alias={}):
    return pl.pallas_call(
        kernel,
        out_shape=outs,
        in_specs=ins,
        out_specs=[VMEM if str(o.memory_space) == "vmem" else HBM for o in outs],
        scratch_shapes=list(scratch),
        input_output_aliases=alias,
        compiler_params=pltpu.CompilerParams(vmem_limit_bytes=mib << 20),
        cost_estimate=pl.CostEstimate(flops=flops, bytes_accessed=mbytes << 20, transcendentals=0),
    )(*[pltpu.with_memory_space_constraint(x, s.memory_space) for x, s in zip(operands, ins)])


def dot(a, b):
    return jnp.dot(a, b, preferred_element_type=F32)


def lanes(index, size):
    return pl.ds(pl.multiple_of(index * size, 128), size)


def forward_kernel(sens_hbm, inv_hbm, coup_hbm, fwd_hbm, fwd1, away, part, coup1, inv, sens, turned, coup0, fwd0, term, sems):
    half = away.shape[0]
    core = lax.axis_index("core")
    fwd = (fwd0, fwd1)
    wide = inv.shape[2] // 2
    columns = [slice(0, wide), slice(wide, 2 * wide)]
    sens_loads = [pltpu.make_async_copy(sens_hbm.at[b], sens.at[b], sems.at[b]) for b in range(2)]
    inv_loads = [[pltpu.make_async_copy(inv_hbm.at[b, :, s], inv.at[b, :, s], sems.at[2 + 2 * b + i]) for i, s in enumerate(columns)] for b in range(2)]
    coup_loads = [pltpu.make_async_copy(coup_hbm.at[b], coup, sems.at[6 + b]) for b, coup in enumerate((coup0, coup1))]
    for load in (sens_loads[0], *inv_loads[0], coup_loads[0], sens_loads[1], *inv_loads[1], coup_loads[1]):
        load.start()
    stores = [pltpu.make_async_copy(fwd[b], fwd_hbm.at[b], sems.at[8 + b]) for b in range(2)]
    for b in range(2):
        sens_loads[b].wait()
        turned[b] = sens[b].T
        for load, s in zip(inv_loads[b], columns):
            load.wait()
            fwd[b][:, s] = dot(turned[b], inv[b, :, s]).astype(BF16)
        stores[b].start()
        coup_loads[b].wait()
        if b == 0:
            term[...] = dot(fwd0[...], coup0[...])
            part[...] = term[lanes(core, half), :]
    away[...] = (term[lanes(1 - core, half), :] + dot(fwd1[lanes(1 - core, half), :], coup1[...])).astype(BF16)
    for store in stores:
        store.wait()


def mine_kernel(part, fwd1, coup1, out):
    out[...] = part[...] + dot(fwd1[lanes(lax.axis_index("core"), out.shape[0]), :], coup1[...])


def order_kernel(ring0, ring1, ring2, ring3, out):
    yed = lax.axis_index("y")
    for step, ring in enumerate((ring0, ring1, ring2, ring3)):
        out[lax.rem(yed + 4 - step, 4)] = ring[...]


def join_kernel(mine, came, out_hbm, out, sems):
    quarter = out.shape[2]
    copies = []
    for z in range(4):
        span = slice(z * quarter, (z + 1) * quarter)
        value = (mine[:, span] + came[:, span].astype(F32)).astype(BF16)
        out[z * 16:(z + 1) * 16] = value.reshape(16, -1, quarter)
        copies.append(pltpu.make_async_copy(out.at[z * 16:(z + 1) * 16], out_hbm.at[z * 16:(z + 1) * 16], sems.at[z]))
        copies[-1].start()
    for copy in copies:
        copy.wait()


def unroll(got, lhs, side):
    half, quarter = lhs.shape[0] // 2, got.shape[2]
    for z in range(4):
        lhs[lanes(side, half), ORDER[z] * quarter:(ORDER[z] + 1) * quarter] = got[z * 16:(z + 1) * 16].reshape(-1, quarter)


def own_kernel(got, coup_hbm, inv_hbm, pulled, coup, inv, lhs, total, sems):
    third = coup.shape[0] // 3
    half = pulled.shape[0]
    core = lax.axis_index("core")
    spans = [slice(i * third, (i + 1) * third) for i in range(3)]
    loads = [pltpu.make_async_copy(coup_hbm.at[0, s, :], coup.at[s, :], sems.at[i]) for i, s in enumerate(spans)]
    loads.append(pltpu.make_async_copy(inv_hbm.at[0], inv, sems.at[3]))
    for load in loads:
        load.start()
    unroll(got, lhs, core)
    for i, s in enumerate(spans):
        loads[i].wait()
        value = dot(lhs[lanes(core, half), s], coup[s, :])
        total[...] = value if i == 0 else total[...] + value
    pulled[...] = total[...].astype(BF16)
    loads[3].wait()


def other_kernel(
    own, other, pulled_own, coup0, inv0, coup_hbm, inv_hbm, fwd_hbm, adjoint_hbm, border_hbm,
    coup1, inv1, fwd, adjoint, border, lhs, pulled, total, sems,
):
    half, quarter = pulled_own.shape[0], own.shape[2]
    third = coup1.shape[0] // 3
    core = lax.axis_index("core")
    zed = lax.axis_index("z")
    spans = [slice(i * third, (i + 1) * third) for i in range(3)]
    fwd_loads = [pltpu.make_async_copy(fwd_hbm.at[b], fwd.at[b], sems.at[b]) for b in range(2)]
    coup_loads = [pltpu.make_async_copy(coup_hbm.at[1, s, :], coup1.at[s, :], sems.at[2 + i]) for i, s in enumerate(spans)]
    inv_load = pltpu.make_async_copy(inv_hbm.at[1], inv1, sems.at[5])
    for load in (fwd_loads[0], *coup_loads, inv_load, fwd_loads[1]):
        load.start()
    unroll(own, lhs, core)
    unroll(other, lhs, 1 - core)
    pulled[0, lanes(core, half), :] = pulled_own[...]
    pulled[0, lanes(1 - core, half), :] = dot(lhs[lanes(1 - core, half), :], coup0[...]).astype(BF16)

    rows = border.shape[0]
    first = (lax.axis_index("y") * 2 + core) * rows
    spot = first + lax.broadcasted_iota(jnp.int32, (rows, quarter), 0)
    pick = (lax.broadcasted_iota(jnp.int32, (rows, quarter), 1) == spot).astype(BF16)
    source = jnp.where(zed == 0, 0, jnp.where(zed == 1, 3, zed - 1))
    for ref, side in ((own, core), (other, 1 - core)):
        chosen = ref[pl.ds(source * 16, 16)].reshape(-1, quarter)
        picked = lax.dot_general(pick, chosen, (((1,), (1,)), ((), ())), preferred_element_type=F32)
        border[:, lanes(side, half)] = picked.astype(BF16)
    stores = [pltpu.make_async_copy(border, border_hbm, sems.at[6])]
    stores[0].start()

    step = inv1.shape[1] // 4

    def finish(b, inv):
        for i in range(4):
            span = slice(i * step, (i + 1) * step)
            value = fwd[b, :, span].astype(F32) - dot(pulled[b], inv[:, span])
            adjoint[b, span, :] = value.astype(BF16).T
            stores.append(pltpu.make_async_copy(adjoint.at[b, span, :], adjoint_hbm.at[b, span, :], sems.at[7 + 4 * b + i]))
            stores[-1].start()

    fwd_loads[0].wait()
    finish(0, inv0)
    for i, s in enumerate(spans):
        coup_loads[i].wait()
        value = dot(lhs[:, s], coup1[s, :])
        total[...] = value if i == 0 else total[...] + value
    pulled[1] = total[...].astype(BF16)
    inv_load.wait()
    fwd_loads[1].wait()
    finish(1, inv1)
    for store in stores:
        store.wait()


def rhs_kernel(rhs_hbm, out, rhs, sem):
    piece, quarter = out.shape
    cols = rhs.shape[1]
    load = pltpu.make_async_copy(rhs_hbm.at[lanes(lax.axis_index("z"), quarter), :], rhs, sem)
    load.start()
    start = lax.axis_index("core") * (cols // 2) + lax.axis_index(("y", "xh", "xl")) * piece
    spot = start + lax.broadcasted_iota(jnp.int32, (piece, cols), 0)
    pick = (lax.broadcasted_iota(jnp.int32, (piece, cols), 1) == spot).astype(BF16)
    load.wait()
    out[...] = lax.dot_general(pick, rhs[...], (((1,), (1,)), ((), ())), preferred_element_type=F32)


def share_kernel(parts, rhs, plane, keep, give):
    zed = lax.axis_index("z")
    residual = (rhs[...] - jnp.sum(parts[...].astype(F32), axis=0)).astype(BF16)
    share = dot(residual, plane[...])
    half = keep.shape[1]
    inner = (zed == 1) | (zed == 2)
    keep[...] = jnp.where(inner, share[:, half:], share[:, :half])
    give[...] = jnp.where(inner, share[:, :half], share[:, half:])


def steps(block_inverse, coupling_in, coupling_out, sensitivities, border_rhs, border_inverse):
    core = lax.axis_index("core")
    zed = lax.axis_index("z")
    rows, link = border_inverse.shape
    n, cols = sensitivities.shape[1:]
    half, quarter = cols // 2, link // 4
    piece = cols // 32
    sem = pltpu.SemaphoreType.DMA

    ring = [border_inverse]
    for step in (1, 2, 3):
        ring.append(lax.ppermute(border_inverse, "y", [(i, (i + step) % 4) for i in range(4)]))
    ring, = call(order_kernel, (pltpu.VMEM((4, rows, link), BF16),), [VMEM] * 4, ring, (), 2)
    other = lax.ppermute(ring, "core", SWAP)
    plane = jnp.where(core == 0, jnp.stack([ring, other], 1), jnp.stack([other, ring], 1)).reshape(quarter, link)

    fwd, fwd1, away, part, coup1 = call(
        forward_kernel,
        (
            pltpu.HBM((2, cols, n), BF16), pltpu.VMEM((cols, n), BF16), pltpu.VMEM((half, link), BF16),
            pltpu.VMEM((half, link), F32), pltpu.VMEM((n, link), BF16),
        ),
        [HBM] * 3, (sensitivities, block_inverse, coupling_in),
        [
            pltpu.VMEM((2, n, n), BF16), pltpu.VMEM((2, n, cols), BF16), pltpu.VMEM((2, cols, n), BF16), pltpu.VMEM((n, link), BF16),
            pltpu.VMEM((cols, n), BF16), pltpu.VMEM((cols, link), F32), sem((10,)),
        ],
        28, 4 * n * cols * (n + link), 17)
    came = lax.ppermute(away, "core", SWAP)
    mine, = call(mine_kernel, (pltpu.VMEM((half, link), F32),), [VMEM] * 3, (part, fwd1, coup1), (), 8, 2 * n * half * link, 7)
    terms, = call(
        join_kernel, (pltpu.HBM((64, piece, quarter), BF16),), [VMEM] * 2, (mine, came),
        [pltpu.VMEM((64, piece, quarter), BF16), sem((4,))], 4, 0, 3)
    parts = lax.all_to_all(terms, CHIPS, 0, 0, tiled=True)
    rhs, = call(
        rhs_kernel, (pltpu.VMEM((piece, quarter), F32),), [HBM], (border_rhs,),
        [pltpu.VMEM((quarter, cols), BF16), pltpu.SemaphoreType.DMA], 2)
    keep, give = call(
        share_kernel, (pltpu.VMEM((piece, 2 * quarter), F32),) * 2, [VMEM] * 3, (parts, rhs, plane), (), 4)
    share = keep + lax.ppermute(give, "z", NEAR)
    outer = zed // 2
    came = lax.ppermute(lax.dynamic_slice_in_dim(share, (1 - outer) * quarter, quarter, 1), "z", FAR)
    solved = (lax.dynamic_slice_in_dim(share, outer * quarter, quarter, 1) + came).astype(BF16)

    spread = jnp.broadcast_to(solved[None], (64,) + solved.shape)
    own = lax.all_to_all(spread, CHIPS, 0, 0, tiled=True)
    other = lax.ppermute(own, "core", SWAP)

    pulled, coup0, inv0 = call(
        own_kernel, (pltpu.VMEM((half, n), BF16), pltpu.VMEM((link, n), BF16), pltpu.VMEM((n, n), BF16)),
        [VMEM] + [HBM] * 2, (own, coupling_out, block_inverse),
        [pltpu.VMEM((cols, link), BF16), pltpu.VMEM((half, n), F32), sem((4,))], 8, 2 * half * n * link, 6)
    return call(
        other_kernel, (pltpu.HBM((2, n, cols), BF16), pltpu.HBM((rows, cols), BF16)), [VMEM] * 5 + [HBM] * 3,
        (own, other, pulled, coup0, inv0, coupling_out, block_inverse, fwd),
        [
            pltpu.VMEM((link, n), BF16), pltpu.VMEM((n, n), BF16), pltpu.VMEM((2, cols, n), BF16), pltpu.VMEM((2, n, cols), BF16),
            pltpu.VMEM((rows, cols), BF16), pltpu.VMEM((cols, link), BF16), pltpu.VMEM((2, cols, n), BF16), pltpu.VMEM((cols, n), F32), sem((15,)),
        ],
        24, 4 * cols * n * (n + link // 2), 16)


def body(*args):
    return tuple(steps(*args))


def solution(mesh):
    mesh = Mesh(mesh.devices.reshape(4, 4, 2, 2, 2), ("z", "y", "core", "xh", "xl"))
    every = ("z", "y", "core", "xh", "xl")
    blocks = P(every, None, None)
    lines = P(("z", "y", "core"), None)
    return jax.shard_map(
        body, mesh=mesh, in_specs=(blocks, blocks, blocks, blocks, P(), lines), out_specs=(blocks, lines), check_vma=False
    )
```

time: 90.8 us -> 88.9 us (0.979)
  Pallas kernels: 20.2 us -> 21.6 us
  matrix products: 1.25 us -> 0 us
  waiting for transfers between devices: 26 us -> 24.8 us
    pallas_call x6 -> x8, Pallas kernels: 20.2 us -> 21.6 us  [call(): pl.pallas_call(kernel, out_shape=outs, in_specs=ins, out_specs=[VMEM if s...]
    dot_general x1 -> x0, matrix products: 1.25 us -> none  [dot(): return jnp.dot(a, b, preferred_element_type=F32)]
    all_to_all x1, waiting for transfers between devices: 15.2 us -> 14 us  [steps(): parts = lax.all_to_all(terms, CHIPS, 0, 0, tiled=True)]
  transfers between devices with their start and end apart: 9 -> 9, of which waited for: 6 -> 6; matrix products, arithmetic and copies ran while one was open for 0% -> 0% of each run, Pallas kernels for 10% -> 7%
where the time goes in v4:
time: 88.9 us; the launch traced here: 88.6 us
  waiting for transfers between devices  24.8 us (28%)
  starting transfers between devices  24.5 us (28%)
  Pallas kernels  21.6 us (24%)
  blocking collectives  16.3 us (18%)
  between operations  0.94 us (1%)
    pallas_call x8, Pallas kernels, call(): pl.pallas_call(kernel, out_shape=outs, in_specs=ins, out_specs=[VMEM if s...  21.6 us
    all_to_all x1, blocking collectives, steps(): own = lax.all_to_all(spread, CHIPS, 0, 0, tiled=True)  16.3 us
    all_to_all x1, waiting for transfers between devices, steps(): parts = lax.all_to_all(terms, CHIPS, 0, 0, tiled=True)  14 us
    all_to_all x1, starting transfers between devices, steps(): parts = lax.all_to_all(terms, CHIPS, 0, 0, tiled=True)  10.6 us
    ppermute x3, starting transfers between devices, steps(): lax.ppermute(border_inverse, 'y', [(i, (i + step) % 4) for i in range(4)])  5.7 us
    ppermute x1, starting transfers between devices, steps(): other = lax.ppermute(own, 'core', SWAP)  4.89 us
    ppermute x3, waiting for transfers between devices, steps(): lax.ppermute(border_inverse, 'y', [(i, (i + step) % 4) for i in range(4)])  4.72 us
    ppermute x1, waiting for transfers between devices, steps(): lax.ppermute(lax.dynamic_slice_in_dim(share, (1 - outer) * quarter, quart...  3.19 us
  transfers between devices with their start and end apart: 9, of which 6 were waited for; matrix products, arithmetic and copies ran while one was open for 0% of the time, Pallas kernels for 7%

profile of v4, /device:TPU:1, one launch (start us, length us, event | category | flops | bytes accessed | tf_op | source)
XLA Modules:
  0.0 88.6 jit_solution(9379159302688366004)
XLA Ops:
  0.6 0.0 copy-start
  0.6 7.9 %shard_map.77 = (bf16[2,512,1024]{2,1,0:T(8,128)(2,1)}, bf16[512,1024]{1,0:T(8,128)(2,1)S(1)}, bf16[256,1536]{1,0:T(8,128)(2,1)S(1)}, f32[256,1536]{1,0:T(8,128)S(1)}, bf16[1024,1536]{1,0:T(8,128)(2,1)S(1)}) custom-call(bf16[2,1024,512]{2,1,0:T(8,128)(2,1)} %sens_hbm.1, bf16[2,1024,1024]{2,1,0:T(8,128)(2,1)} %inv_hbm.5, bf16[2,1024,1536]{2,1,0:T(8,128)(2,1)} %coup_hbm.3), custom_call_target="tpu_custom_call" | custom-call | flops 5368709120 | bytes 17825792 | tf_op jit(solution)/shard_map/pallas_call | solution.py:20
  8.5 1.4 %collective-permute-start = (bf16[256,1536]{1,0:T(8,128)(2,1)S(1)}, bf16[256,1536]{1,0:T(8,128)(2,1)S(1)}, u32[]{:S(2)}, u32[]{:S(2)}) collective-permute-start(bf16[256,1536]{1,0:T(8,128)(2,1)S(1)} %get-tuple-element.15), channel_id=1, source_target_pairs={{0,4},{4,0},{1,5},{5,1},{2,6},{6,2},{3,7},{7,3},{8,12},{12,8},{9,1... | collective-permute-start | bytes 2359304 | tf_op jit(solution)/shard_map/ppermute | solution.py:220
  9.9 0.0 copy-done
  9.9 3.0 %collective-permute-start.2 = (bf16[48,1536]{1,0:T(8,128)(2,1)S(1)}, bf16[48,1536]{1,0:T(8,128)(2,1)S(1)}, u32[]{:S(2)}, u32[]{:S(2)}) collective-permute-start(bf16[48,1536]{1,0:T(8,128)(2,1)S(1)} %copy-done), channel_id=1, source_target_pairs={{0,16},{8,24},{16,0},{24,8},{1,17},{9,25},{17,1},{25,9},{2,18},{10... | collective-permute-start | bytes 442376 | tf_op jit(solution)/shard_map/ppermute | solution.py:203
  13.0 0.4 collective-permute-start.1
  13.4 2.3 %collective-permute-start.3 = (bf16[48,1536]{1,0:T(8,128)(2,1)S(1)}, bf16[48,1536]{1,0:T(8,128)(2,1)S(1)}, u32[]{:S(2)}, u32[]{:S(2)}) collective-permute-start(bf16[48,1536]{1,0:T(8,128)(2,1)S(1)} %copy-done), channel_id=1, source_target_pairs={{0,24},{8,0},{16,8},{24,16},{1,25},{9,1},{17,9},{25,17},{2,26},{10... | collective-permute-start | bytes 442376 | tf_op jit(solution)/shard_map/ppermute | solution.py:203
  15.6 1.2 %collective-permute-done.2.ring2 = bf16[48,1536]{1,0:T(8,128)(2,1)S(1)} collective-permute-done((bf16[48,1536]{1,0:T(8,128)(2,1)S(1)}, bf16[48,1536]{1,0:T(8,128)(2,1)S(1)}, u32[]{:S(2)}, u32[]{:S(2)}) %collective-permute-start.2) | collective-permute-done | bytes 147488 | tf_op jit(solution)/shard_map/ppermute | solution.py:203
  16.9 3.2 %collective-permute-done.1.ring1 = bf16[48,1536]{1,0:T(8,128)(2,1)S(1)} collective-permute-done((bf16[48,1536]{1,0:T(8,128)(2,1)S(1)}, bf16[48,1536]{1,0:T(8,128)(2,1)S(1)}, u32[]{:S(2)}, u32[]{:S(2)}) %collective-permute-start.1) | collective-permute-done | bytes 147488 | tf_op jit(solution)/shard_map/ppermute | solution.py:203
  20.1 0.2 collective-permute-done.3.ring3
  20.4 0.1 shard_map.81
  20.4 1.0 %collective-permute-start.4 = (bf16[4,48,1536]{2,1,0:T(8,128)(2,1)S(1)}, bf16[4,48,1536]{2,1,0:T(8,128)(2,1)S(1)}, u32[]{:S(2)}, u32[]{:S(2)}) collective-permute-start(bf16[4,48,1536]{2,1,0:T(8,128)(2,1)S(1)} %shard_map.81), channel_id=1, source_target_pairs={{0,4},{4,0},{1,5},{5,1},{2,6},{6,2},{3,7},{7,3},{8,12},{12,8},{9,1... | collective-permute-start | bytes 1769480 | tf_op jit(solution)/shard_map/ppermute | solution.py:205
  21.5 1.0 %shard_map.78.mine = f32[256,1536]{1,0:T(8,128)S(1)} custom-call(f32[256,1536]{1,0:T(8,128)S(1)} %get-tuple-element.12.part, bf16[512,1024]{1,0:T(8,128)(2,1)S(1)} %get-tuple-element.13.fwd1, bf16[1024,1536]{1,0:T(8,128)(2,1)S(1)} %get-tuple-element.14.coup1), custom_call_target="tpu_custom_call" | custom-call | flops 805306368 | bytes 7340032 | tf_op jit(solution)/shard_map/pallas_call | solution.py:20
  22.4 0.0 collective-permute-done.came
  22.4 0.9 %shard_map.79 = bf16[64,16,384]{2,1,0:T(8,128)(2,1)} custom-call(f32[256,1536]{1,0:T(8,128)S(1)} %shard_map.78.mine, bf16[256,1536]{1,0:T(8,128)(2,1)S(1)} %collective-permute-done.came), custom_call_target="tpu_custom_call" | custom-call | bytes 3145728 | tf_op jit(solution)/shard_map/pallas_call | solution.py:20
  23.4 10.6 %all-to-all-start = ((bf16[64,16,384]{2,1,0:T(8,128)(2,1)}), bf16[64,16,384]{2,1,0:T(8,128)(2,1)S(1)}, u32[]{:S(2)}, u32[]{:S(2)}) async-start(bf16[64,16,384]{2,1,0:T(8,128)(2,1)} %shard_map.79), calls=%async_computation | async-start | bytes 1572864 | tf_op jit(solution)/shard_map/all_to_all | solution.py:225
  34.0 1.3 %shard_map.80.rhs = f32[16,384]{1,0:T(8,128)S(1)} custom-call(bf16[1536,512]{1,0:T(8,128)(2,1)} %rhs_hbm.1), custom_call_target="tpu_custom_call" | custom-call | bytes 1048576 | tf_op jit(solution)/shard_map/pallas_call | solution.py:20
  35.3 0.0 collective-permute-done.4
  35.3 0.2 maximum_select_fusion
  35.5 0.1 copy.8
  35.6 14.0 %all-to-all-done.parts = bf16[64,16,384]{2,1,0:T(8,128)(2,1)S(1)} async-done(((bf16[64,16,384]{2,1,0:T(8,128)(2,1)}), bf16[64,16,384]{2,1,0:T(8,128)(2,1)S(1)}, u32[]{:S(2)}, u32[]{:S(2)}) %all-to-all-start) | async-done | bytes 786464 | tf_op jit(solution)/shard_map/all_to_all | solution.py:225
  49.6 0.4 shard_map.82
  49.9 0.0 collective-permute-start.5
  50.0 2.9 %collective-permute-done.5 = f32[16,768]{1,0:T(8,128)S(1)} collective-permute-done((f32[16,768]{1,0:T(8,128)S(1)}, f32[16,768]{1,0:T(8,128)S(1)}, u32[]{:S(2)}, u32[]{:S(2)}) %collective-permute-start.5) | collective-permute-done | bytes 49184 | tf_op jit(solution)/shard_map/ppermute | solution.py:231
  52.9 0.8 collective-permute-start.6
  53.7 3.2 %collective-permute-done.6 = f32[16,384]{1,0:T(8,128)S(1)} collective-permute-done((f32[16,384]{1,0:T(8,128)S(1)}, f32[16,384]{1,0:T(8,128)S(1)}, u32[]{:S(2)}, u32[]{:S(2)}) %collective-permute-start.6) | collective-permute-done | bytes 24608 | tf_op jit(solution)/shard_map/ppermute | solution.py:233
  56.9 0.1 broadcast_in_dim.2
  57.0 16.3 %all_to_all.10.got.own = bf16[64,16,384]{2,1,0:T(8,128)(2,1)S(1)} all-to-all(bf16[64,16,384]{2,1,0:T(8,128)(2,1)S(1)} %broadcast_in_dim.2), channel_id=1, replica_groups=mesh['z'=4,'y'=4,'core'=2,'xh'=2,'xl'=2] {'z','y','xh','xl'}, dimensions={0} | all-to-all | bytes 1572864 | tf_op jit(solution)/shard_map/all_to_all | solution.py:237
  73.3 4.9 %collective-permute-start.7 = (bf16[64,16,384]{2,1,0:T(8,128)(2,1)S(1)}, bf16[64,16,384]{2,1,0:T(8,128)(2,1)S(1)}, u32[]{:S(2)}, u32[]{:S(2)}) collective-permute-start(bf16[64,16,384]{2,1,0:T(8,128)(2,1)S(1)} %all_to_all.10.got.own), channel_id=1, source_target_pairs={{0,4},{4,0},{1,5},{5,1},{2,6},{6,2},{3,7},{7,3},{8,12},{12,8},{9,1... | collective-permute-start | bytes 2359304 | tf_op jit(solution)/shard_map/ppermute | solution.py:238
  78.2 2.6 %shard_map.83 = (bf16[256,1024]{1,0:T(8,128)(2,1)S(1)}, bf16[1536,1024]{1,0:T(8,128)(2,1)S(1)}, bf16[1024,1024]{1,0:T(8,128)(2,1)S(1)}) custom-call(bf16[64,16,384]{2,1,0:T(8,128)(2,1)S(1)} %all_to_all.10.got.own, bf16[2,1536,1024]{2,1,0:T(8,128)(2,1)} %coup_hbm.5, bf16[2,1024,1024]{2,1,0:T(8,128)(2,1)} %inv_hbm.5), custom_call_target="tpu_custom_call" | custom-call | flops 805306368 | bytes 6291456 | tf_op jit(solution)/shard_map/pallas_call | solution.py:20
  80.8 0.0 collective-permute-done.7.other
  80.8 7.6 %shard_map.84 = (bf16[2,1024,512]{2,1,0:T(8,128)(2,1)}, bf16[48,512]{1,0:T(8,128)(2,1)}) custom-call(bf16[64,16,384]{2,1,0:T(8,128)(2,1)S(1)} %all_to_all.10.got.own, bf16[64,16,384]{2,1,0:T(8,128)(2,1)S(1)} %collective-permute-done.7.other, bf16[256,1024]{1,0:T(8,128)(2,1)S(1)} %get-tuple-element.18.pulled_own, ...), custom_call_target="tpu_custom_call" | custom-call | flops 3758096384 | bytes 16777216 | tf_op jit(solution)/shard_map/pallas_call | solution.py:20
  (3 shorter events, 0.0 us)
Async XLA Ops:
  0.6 9.3 %copy-start = (bf16[48,1536]{1,0:T(8,128)(2,1)S(1)}, bf16[48,1536]{1,0:T(8,128)(2,1)}, u32[]{:S(2)}) copy-start(bf16[48,1536]{1,0:T(8,128)(2,1)} %ring0.1) | copy-start | bytes 442372
  8.5 13.9 %collective-permute-start = (bf16[256,1536]{1,0:T(8,128)(2,1)S(1)}, bf16[256,1536]{1,0:T(8,128)(2,1)S(1)}, u32[]{:S(2)}, u32[]{:S(2)}) collective-permute-start(bf16[256,1536]{1,0:T(8,128)(2,1)S(1)} %get-tuple-element.15), channel_id=1, source_target_pairs={{0,4},{4,0},{1,5},{5,1},{2,6},{6,2},{3,7},{7,3},{8,12},{12,8},{9,1... | collective-permute-start | bytes 2359304 | tf_op jit(solution)/shard_map/ppermute | solution.py:220
  9.9 6.9 %collective-permute-start.2 = (bf16[48,1536]{1,0:T(8,128)(2,1)S(1)}, bf16[48,1536]{1,0:T(8,128)(2,1)S(1)}, u32[]{:S(2)}, u32[]{:S(2)}) collective-permute-start(bf16[48,1536]{1,0:T(8,128)(2,1)S(1)} %copy-done), channel_id=1, source_target_pairs={{0,16},{8,24},{16,0},{24,8},{1,17},{9,25},{17,1},{25,9},{2,18},{10... | collective-permute-start | bytes 442376 | tf_op jit(solution)/shard_map/ppermute | solution.py:203
  13.0 7.2 %collective-permute-start.1 = (bf16[48,1536]{1,0:T(8,128)(2,1)S(1)}, bf16[48,1536]{1,0:T(8,128)(2,1)S(1)}, u32[]{:S(2)}, u32[]{:S(2)}) collective-permute-start(bf16[48,1536]{1,0:T(8,128)(2,1)S(1)} %copy-done), channel_id=1, source_target_pairs={{0,8},{8,16},{16,24},{24,0},{1,9},{9,17},{17,25},{25,1},{2,10},{10... | collective-permute-start | bytes 442376 | tf_op jit(solution)/shard_map/ppermute | solution.py:203
  13.4 7.0 %collective-permute-start.3 = (bf16[48,1536]{1,0:T(8,128)(2,1)S(1)}, bf16[48,1536]{1,0:T(8,128)(2,1)S(1)}, u32[]{:S(2)}, u32[]{:S(2)}) collective-permute-start(bf16[48,1536]{1,0:T(8,128)(2,1)S(1)} %copy-done), channel_id=1, source_target_pairs={{0,24},{8,0},{16,8},{24,16},{1,25},{9,1},{17,9},{25,17},{2,26},{10... | collective-permute-start | bytes 442376 | tf_op jit(solution)/shard_map/ppermute | solution.py:203
  20.4 14.9 %collective-permute-start.4 = (bf16[4,48,1536]{2,1,0:T(8,128)(2,1)S(1)}, bf16[4,48,1536]{2,1,0:T(8,128)(2,1)S(1)}, u32[]{:S(2)}, u32[]{:S(2)}) collective-permute-start(bf16[4,48,1536]{2,1,0:T(8,128)(2,1)S(1)} %shard_map.81), channel_id=1, source_target_pairs={{0,4},{4,0},{1,5},{5,1},{2,6},{6,2},{3,7},{7,3},{8,12},{12,8},{9,1... | collective-permute-start | bytes 1769480 | tf_op jit(solution)/shard_map/ppermute | solution.py:205
  23.4 26.2 %all-to-all-start = ((bf16[64,16,384]{2,1,0:T(8,128)(2,1)}), bf16[64,16,384]{2,1,0:T(8,128)(2,1)S(1)}, u32[]{:S(2)}, u32[]{:S(2)}) async-start(bf16[64,16,384]{2,1,0:T(8,128)(2,1)} %shard_map.79), calls=%async_computation | async-start | bytes 1572864 | tf_op jit(solution)/shard_map/all_to_all | solution.py:225
  49.9 3.0 %collective-permute-start.5 = (f32[16,768]{1,0:T(8,128)S(1)}, f32[16,768]{1,0:T(8,128)S(1)}, u32[]{:S(2)}, u32[]{:S(2)}) collective-permute-start(f32[16,768]{1,0:T(8,128)S(1)} %get-tuple-element.17), channel_id=1, source_target_pairs={{0,32},{32,0},{64,96},{96,64},{1,33},{33,1},{65,97},{97,65},{2,34}... | collective-permute-start | bytes 147464 | tf_op jit(solution)/shard_map/ppermute | solution.py:231
  52.9 4.0 %collective-permute-start.6 = (f32[16,384]{1,0:T(8,128)S(1)}, f32[16,384]{1,0:T(8,128)S(1)}, u32[]{:S(2)}, u32[]{:S(2)}) collective-permute-start(f32[16,384]{1,0:T(8,128)S(1)} %constant_dynamic-slice_fusion), channel_id=1, source_target_pairs={{0,96},{96,0},{32,64},{64,32},{1,97},{97,1},{33,65},{65,33},{2,98}... | collective-permute-start | bytes 73736 | tf_op jit(solution)/shard_map/ppermute | solution.py:233
  73.3 7.5 %collective-permute-start.7 = (bf16[64,16,384]{2,1,0:T(8,128)(2,1)S(1)}, bf16[64,16,384]{2,1,0:T(8,128)(2,1)S(1)}, u32[]{:S(2)}, u32[]{:S(2)}) collective-permute-start(bf16[64,16,384]{2,1,0:T(8,128)(2,1)S(1)} %all_to_all.10.got.own), channel_id=1, source_target_pairs={{0,4},{4,0},{1,5},{5,1},{2,6},{6,2},{3,7},{7,3},{8,12},{12,8},{9,1... | collective-permute-start | bytes 2359304 | tf_op jit(solution)/shard_map/ppermute | solution.py:238

commit v5 on v4

--- a/solution.py
+++ b/solution.py
@@ -33,40 +33,46 @@
     return jnp.dot(a, b, preferred_element_type=F32)
 
 
+def long_dot(a, b):
+    cut = b.shape[0] * 2 // 3
+    return dot(a[:, :cut], b[:cut]) + dot(a[:, cut:], b[cut:])
+
+
 def lanes(index, size):
     return pl.ds(pl.multiple_of(index * size, 128), size)
 
 
-def forward_kernel(sens_hbm, inv_hbm, coup_hbm, fwd_hbm, fwd1, away, part, coup1, inv, sens, turned, coup0, fwd0, term, sems):
+def forward_kernel(sens_hbm, inv_hbm, coup_hbm, fwd_hbm, fwd1, away, term, coup1, inv, sens, turned, coup0, fwd0, sems):
     half = away.shape[0]
     core = lax.axis_index("core")
-    fwd = (fwd0, fwd1)
-    wide = inv.shape[2] // 2
-    columns = [slice(0, wide), slice(wide, 2 * wide)]
+    fwd, coup = (fwd0, fwd1), (coup0, coup1)
     sens_loads = [pltpu.make_async_copy(sens_hbm.at[b], sens.at[b], sems.at[b]) for b in range(2)]
-    inv_loads = [[pltpu.make_async_copy(inv_hbm.at[b, :, s], inv.at[b, :, s], sems.at[2 + 2 * b + i]) for i, s in enumerate(columns)] for b in range(2)]
-    coup_loads = [pltpu.make_async_copy(coup_hbm.at[b], coup, sems.at[6 + b]) for b, coup in enumerate((coup0, coup1))]
-    for load in (sens_loads[0], *inv_loads[0], coup_loads[0], sens_loads[1], *inv_loads[1], coup_loads[1]):
+    inv_loads = [pltpu.make_async_copy(inv_hbm.at[b], inv.at[b], sems.at[2 + b]) for b in range(2)]
+    coup_loads = [pltpu.make_async_copy(coup_hbm.at[b], coup[b], sems.at[4 + b]) for b in range(2)]
+    for load in (sens_loads[0], inv_loads[0], sens_loads[1], coup_loads[0], inv_loads[1], coup_loads[1]):
         load.start()
-    stores = [pltpu.make_async_copy(fwd[b], fwd_hbm.at[b], sems.at[8 + b]) for b in range(2)]
-    for b in range(2):
-        sens_loads[b].wait()
-        turned[b] = sens[b].T
-        for load, s in zip(inv_loads[b], columns):
-            load.wait()
-            fwd[b][:, s] = dot(turned[b], inv[b, :, s]).astype(BF16)
-        stores[b].start()
-        coup_loads[b].wait()
-        if b == 0:
-            term[...] = dot(fwd0[...], coup0[...])
-            part[...] = term[lanes(core, half), :]
+    stores = [pltpu.make_async_copy(fwd[b], fwd_hbm.at[b], sems.at[6 + b]) for b in range(2)]
+    sens_loads[0].wait()
+    turned[0] = sens[0].T
+    inv_loads[0].wait()
+    sens_loads[1].wait()
+    fwd0[...] = dot(turned[0], inv[0]).astype(BF16)
+    turned[1] = sens[1].T
+    coup_loads[0].wait()
+    term[...] = dot(fwd0[...], coup0[...])
+    inv_loads[1].wait()
+    stores[0].start()
+    fwd1[...] = dot(turned[1], inv[1]).astype(BF16)
+    coup_loads[1].wait()
+    stores[1].start()
     away[...] = (term[lanes(1 - core, half), :] + dot(fwd1[lanes(1 - core, half), :], coup1[...])).astype(BF16)
     for store in stores:
         store.wait()
 
 
-def mine_kernel(part, fwd1, coup1, out):
-    out[...] = part[...] + dot(fwd1[lanes(lax.axis_index("core"), out.shape[0]), :], coup1[...])
+def mine_kernel(term, fwd1, coup1, out):
+    rows = lanes(lax.axis_index("core"), out.shape[0])
+    out[...] = term[rows, :] + dot(fwd1[rows, :], coup1[...])
 
 
 def order_kernel(ring0, ring1, ring2, ring3, out):
@@ -75,17 +81,12 @@
         out[lax.rem(yed + 4 - step, 4)] = ring[...]
 
 
-def join_kernel(mine, came, out_hbm, out, sems):
+def join_kernel(mine, came, out):
     quarter = out.shape[2]
-    copies = []
     for z in range(4):
         span = slice(z * quarter, (z + 1) * quarter)
         value = (mine[:, span] + came[:, span].astype(F32)).astype(BF16)
         out[z * 16:(z + 1) * 16] = value.reshape(16, -1, quarter)
-        copies.append(pltpu.make_async_copy(out.at[z * 16:(z + 1) * 16], out_hbm.at[z * 16:(z + 1) * 16], sems.at[z]))
-        copies[-1].start()
-    for copy in copies:
-        copy.wait()
 
 
 def unroll(got, lhs, side):
@@ -114,57 +115,58 @@
 
 def other_kernel(
     own, other, pulled_own, coup0, inv0, coup_hbm, inv_hbm, fwd_hbm, adjoint_hbm, border_hbm,
-    coup1, inv1, fwd, adjoint, border, lhs, pulled, total, sems,
+    coup1, inv1, fwd, adjoint, border, lhs, pulled, value, sems,
 ):
     half, quarter = pulled_own.shape[0], own.shape[2]
-    third = coup1.shape[0] // 3
     core = lax.axis_index("core")
     zed = lax.axis_index("z")
-    spans = [slice(i * third, (i + 1) * third) for i in range(3)]
     fwd_loads = [pltpu.make_async_copy(fwd_hbm.at[b], fwd.at[b], sems.at[b]) for b in range(2)]
-    coup_loads = [pltpu.make_async_copy(coup_hbm.at[1, s, :], coup1.at[s, :], sems.at[2 + i]) for i, s in enumerate(spans)]
-    inv_load = pltpu.make_async_copy(inv_hbm.at[1], inv1, sems.at[5])
-    for load in (fwd_loads[0], *coup_loads, inv_load, fwd_loads[1]):
+    coup_load = pltpu.make_async_copy(coup_hbm.at[1], coup1, sems.at[2])
+    inv_load = pltpu.make_async_copy(inv_hbm.at[1], inv1, sems.at[3])
+    for load in (fwd_loads[0], coup_load, inv_load, fwd_loads[1]):
         load.start()
+    step = inv1.shape[1] // 4
+    spans = [slice(i * step, (i + 1) * step) for i in range(4)]
+    stores = []
+
+    def store(b, i):
+        stores.append(pltpu.make_async_copy(adjoint.at[b, spans[i], :], adjoint_hbm.at[b, spans[i], :], sems.at[5 + 4 * b + i]))
+        stores[-1].start()
+
     unroll(own, lhs, core)
     unroll(other, lhs, 1 - core)
     pulled[0, lanes(core, half), :] = pulled_own[...]
-    pulled[0, lanes(1 - core, half), :] = dot(lhs[lanes(1 - core, half), :], coup0[...]).astype(BF16)
+    pulled[0, lanes(1 - core, half), :] = long_dot(lhs[lanes(1 - core, half), :], coup0).astype(BF16)
+    fwd_loads[0].wait()
+    for i in range(2):
+        s = slice(2 * i * step, 2 * (i + 1) * step)
+        value[:, s] = (fwd[0, :, s].astype(F32) - dot(pulled[0], inv0[:, s])).astype(BF16)
 
     rows = border.shape[0]
     first = (lax.axis_index("y") * 2 + core) * rows
     spot = first + lax.broadcasted_iota(jnp.int32, (rows, quarter), 0)
     pick = (lax.broadcasted_iota(jnp.int32, (rows, quarter), 1) == spot).astype(BF16)
     source = jnp.where(zed == 0, 0, jnp.where(zed == 1, 3, zed - 1))
+    coup_load.wait()
     for ref, side in ((own, core), (other, 1 - core)):
         chosen = ref[pl.ds(source * 16, 16)].reshape(-1, quarter)
         picked = lax.dot_general(pick, chosen, (((1,), (1,)), ((), ())), preferred_element_type=F32)
         border[:, lanes(side, half)] = picked.astype(BF16)
-    stores = [pltpu.make_async_copy(border, border_hbm, sems.at[6])]
+    for s in spans:
+        adjoint[0, s, :] = value[:, s].T
+    pulled[1] = long_dot(lhs, coup1).astype(BF16)
+    stores.append(pltpu.make_async_copy(border, border_hbm, sems.at[4]))
     stores[0].start()
-
-    step = inv1.shape[1] // 4
-
-    def finish(b, inv):
-        for i in range(4):
-            span = slice(i * step, (i + 1) * step)
-            value = fwd[b, :, span].astype(F32) - dot(pulled[b], inv[:, span])
-            adjoint[b, span, :] = value.astype(BF16).T
-            stores.append(pltpu.make_async_copy(adjoint.at[b, span, :], adjoint_hbm.at[b, span, :], sems.at[7 + 4 * b + i]))
-            stores[-1].start()
-
-    fwd_loads[0].wait()
-    finish(0, inv0)
-    for i, s in enumerate(spans):
-        coup_loads[i].wait()
-        value = dot(lhs[:, s], coup1[s, :])
-        total[...] = value if i == 0 else total[...] + value
-    pulled[1] = total[...].astype(BF16)
+    for i in range(4):
+        store(0, i)
     inv_load.wait()
     fwd_loads[1].wait()
-    finish(1, inv1)
-    for store in stores:
-        store.wait()
+    for i, s in enumerate(spans):
+        for rows in (slice(0, half), slice(half, 2 * half)) if i > 1 else (slice(0, 2 * half),):
+            adjoint[1, s, rows] = (fwd[1, rows, s].astype(F32) - dot(pulled[1, rows, :], inv1[:, s])).astype(BF16).T
+        store(1, i)
+    for copy in stores:
+        copy.wait()
 
 
 def rhs_kernel(rhs_hbm, out, rhs, sem):
@@ -205,23 +207,21 @@
     other = lax.ppermute(ring, "core", SWAP)
     plane = jnp.where(core == 0, jnp.stack([ring, other], 1), jnp.stack([other, ring], 1)).reshape(quarter, link)
 
-    fwd, fwd1, away, part, coup1 = call(
+    fwd, fwd1, away, term, coup1 = call(
         forward_kernel,
         (
             pltpu.HBM((2, cols, n), BF16), pltpu.VMEM((cols, n), BF16), pltpu.VMEM((half, link), BF16),
-            pltpu.VMEM((half, link), F32), pltpu.VMEM((n, link), BF16),
+            pltpu.VMEM((cols, link), F32), pltpu.VMEM((n, link), BF16),
         ),
         [HBM] * 3, (sensitivities, block_inverse, coupling_in),
         [
             pltpu.VMEM((2, n, n), BF16), pltpu.VMEM((2, n, cols), BF16), pltpu.VMEM((2, cols, n), BF16), pltpu.VMEM((n, link), BF16),
-            pltpu.VMEM((cols, n), BF16), pltpu.VMEM((cols, link), F32), sem((10,)),
+            pltpu.VMEM((cols, n), BF16), sem((8,)),
         ],
-        28, 4 * n * cols * (n + link), 17)
+        24, 4 * n * cols * (n + link), 17)
     came = lax.ppermute(away, "core", SWAP)
-    mine, = call(mine_kernel, (pltpu.VMEM((half, link), F32),), [VMEM] * 3, (part, fwd1, coup1), (), 8, 2 * n * half * link, 7)
-    terms, = call(
-        join_kernel, (pltpu.HBM((64, piece, quarter), BF16),), [VMEM] * 2, (mine, came),
-        [pltpu.VMEM((64, piece, quarter), BF16), sem((4,))], 4, 0, 3)
+    mine, = call(mine_kernel, (pltpu.VMEM((half, link), F32),), [VMEM] * 3, (term, fwd1, coup1), (), 8, 2 * n * half * link, 7)
+    terms, = call(join_kernel, (pltpu.VMEM((64, piece, quarter), BF16),), [VMEM] * 2, (mine, came), (), 4, 0, 3)
     parts = lax.all_to_all(terms, CHIPS, 0, 0, tiled=True)
     rhs, = call(
         rhs_kernel, (pltpu.VMEM((piece, quarter), F32),), [HBM], (border_rhs,),
@@ -246,7 +246,7 @@
         (own, other, pulled, coup0, inv0, coupling_out, block_inverse, fwd),
         [
             pltpu.VMEM((link, n), BF16), pltpu.VMEM((n, n), BF16), pltpu.VMEM((2, cols, n), BF16), pltpu.VMEM((2, n, cols), BF16),
-            pltpu.VMEM((rows, cols), BF16), pltpu.VMEM((cols, link), BF16), pltpu.VMEM((2, cols, n), BF16), pltpu.VMEM((cols, n), F32), sem((15,)),
+            pltpu.VMEM((rows, cols), BF16), pltpu.VMEM((cols, link), BF16), pltpu.VMEM((2, cols, n), BF16), pltpu.VMEM((cols, n), BF16), sem((13,)),
         ],
         24, 4 * cols * n * (n + link // 2), 16)
 

time: 88.9 us -> 88.5 us (level)
  waiting for transfers between devices: 24.8 us -> 26 us
  Pallas kernels: 21.6 us -> 20.7 us
    ppermute x3, waiting for transfers between devices: 4.72 us -> 5.94 us  [steps(): lax.ppermute(border_inverse, 'y', [(i, (i + step) % 4) for i in range(4)])]
    pallas_call x8, Pallas kernels: 21.6 us -> 20.7 us  [call(): pl.pallas_call(kernel, out_shape=outs, in_specs=ins, out_specs=[VMEM if s...]
  transfers between devices with their start and end apart: 9 -> 9, of which waited for: 6 -> 5; matrix products, arithmetic and copies ran while one was open for 0% -> 0% of each run, Pallas kernels for 7% -> 7%
where the time goes in v5:
time: 88.5 us; the launch traced here: 88.2 us
  waiting for transfers between devices  26 us (29%)
  starting transfers between devices  23.8 us (27%)
  Pallas kernels  20.7 us (23%)
  blocking collectives  16.3 us (18%)
  between operations  0.94 us (1%)
    pallas_call x8, Pallas kernels, call(): pl.pallas_call(kernel, out_shape=outs, in_specs=ins, out_specs=[VMEM if s...  20.7 us
    all_to_all x1, blocking collectives, steps(): own = lax.all_to_all(spread, CHIPS, 0, 0, tiled=True)  16.3 us
    all_to_all x1, waiting for transfers between devices, steps(): parts = lax.all_to_all(terms, CHIPS, 0, 0, tiled=True)  14 us
    all_to_all x1, starting transfers between devices, steps(): parts = lax.all_to_all(terms, CHIPS, 0, 0, tiled=True)  10.5 us
    ppermute x3, waiting for transfers between devices, steps(): lax.ppermute(border_inverse, 'y', [(i, (i + step) % 4) for i in range(4)])  5.94 us
    ppermute x3, starting transfers between devices, steps(): lax.ppermute(border_inverse, 'y', [(i, (i + step) % 4) for i in range(4)])  5.1 us
    ppermute x1, starting transfers between devices, steps(): other = lax.ppermute(own, 'core', SWAP)  4.89 us
    ppermute x1, waiting for transfers between devices, steps(): lax.ppermute(lax.dynamic_slice_in_dim(share, (1 - outer) * quarter, quart...  3.19 us
  transfers between devices with their start and end apart: 9, of which 5 were waited for; matrix products, arithmetic and copies ran while one was open for 0% of the time, Pallas kernels for 7%

profile of v5, /device:TPU:1, one launch (start us, length us, event | category | flops | bytes accessed | tf_op | source)
XLA Modules:
  0.0 88.2 jit_solution(4693209430833874924)
XLA Ops:
  0.6 0.0 copy-start
  0.6 7.6 %shard_map.77 = (bf16[2,512,1024]{2,1,0:T(8,128)(2,1)}, bf16[512,1024]{1,0:T(8,128)(2,1)S(1)}, bf16[256,1536]{1,0:T(8,128)(2,1)S(1)}, f32[512,1536]{1,0:T(8,128)S(1)}, bf16[1024,1536]{1,0:T(8,128)(2,1)S(1)}) custom-call(bf16[2,1024,512]{2,1,0:T(8,128)(2,1)} %sens_hbm.1, bf16[2,1024,1024]{2,1,0:T(8,128)(2,1)} %inv_hbm.5, bf16[2,1024,1536]{2,1,0:T(8,128)(2,1)} %coup_hbm.3), custom_call_target="tpu_custom_call" | custom-call | flops 5368709120 | bytes 17825792 | tf_op jit(solution)/shard_map/pallas_call | solution.py:20
  8.2 1.5 %collective-permute-start = (bf16[256,1536]{1,0:T(8,128)(2,1)S(1)}, bf16[256,1536]{1,0:T(8,128)(2,1)S(1)}, u32[]{:S(2)}, u32[]{:S(2)}) collective-permute-start(bf16[256,1536]{1,0:T(8,128)(2,1)S(1)} %get-tuple-element.15), channel_id=1, source_target_pairs={{0,4},{4,0},{1,5},{5,1},{2,6},{6,2},{3,7},{7,3},{8,12},{12,8},{9,1... | collective-permute-start | bytes 2359304 | tf_op jit(solution)/shard_map/ppermute | solution.py:222
  9.7 0.0 copy-done
  9.7 1.4 %collective-permute-start.1 = (bf16[48,1536]{1,0:T(8,128)(2,1)S(1)}, bf16[48,1536]{1,0:T(8,128)(2,1)S(1)}, u32[]{:S(2)}, u32[]{:S(2)}) collective-permute-start(bf16[48,1536]{1,0:T(8,128)(2,1)S(1)} %copy-done), channel_id=1, source_target_pairs={{0,8},{8,16},{16,24},{24,0},{1,9},{9,17},{17,25},{25,1},{2,10},{10... | collective-permute-start | bytes 442376 | tf_op jit(solution)/shard_map/ppermute | solution.py:205
  11.1 2.6 %collective-permute-start.2 = (bf16[48,1536]{1,0:T(8,128)(2,1)S(1)}, bf16[48,1536]{1,0:T(8,128)(2,1)S(1)}, u32[]{:S(2)}, u32[]{:S(2)}) collective-permute-start(bf16[48,1536]{1,0:T(8,128)(2,1)S(1)} %copy-done), channel_id=1, source_target_pairs={{0,16},{8,24},{16,0},{24,8},{1,17},{9,25},{17,1},{25,9},{2,18},{10... | collective-permute-start | bytes 442376 | tf_op jit(solution)/shard_map/ppermute | solution.py:205
  13.7 1.1 %collective-permute-start.3 = (bf16[48,1536]{1,0:T(8,128)(2,1)S(1)}, bf16[48,1536]{1,0:T(8,128)(2,1)S(1)}, u32[]{:S(2)}, u32[]{:S(2)}) collective-permute-start(bf16[48,1536]{1,0:T(8,128)(2,1)S(1)} %copy-done), channel_id=1, source_target_pairs={{0,24},{8,0},{16,8},{24,16},{1,25},{9,1},{17,9},{25,17},{2,26},{10... | collective-permute-start | bytes 442376 | tf_op jit(solution)/shard_map/ppermute | solution.py:205
  14.8 1.8 %collective-permute-done.1.ring1 = bf16[48,1536]{1,0:T(8,128)(2,1)S(1)} collective-permute-done((bf16[48,1536]{1,0:T(8,128)(2,1)S(1)}, bf16[48,1536]{1,0:T(8,128)(2,1)S(1)}, u32[]{:S(2)}, u32[]{:S(2)}) %collective-permute-start.1) | collective-permute-done | bytes 147488 | tf_op jit(solution)/shard_map/ppermute | solution.py:205
  16.6 4.2 %collective-permute-done.2.ring2 = bf16[48,1536]{1,0:T(8,128)(2,1)S(1)} collective-permute-done((bf16[48,1536]{1,0:T(8,128)(2,1)S(1)}, bf16[48,1536]{1,0:T(8,128)(2,1)S(1)}, u32[]{:S(2)}, u32[]{:S(2)}) %collective-permute-start.2) | collective-permute-done | bytes 147488 | tf_op jit(solution)/shard_map/ppermute | solution.py:205
  20.7 0.0 collective-permute-done.3.ring3
  20.8 0.1 shard_map.81
  20.8 1.0 %collective-permute-start.4 = (bf16[4,48,1536]{2,1,0:T(8,128)(2,1)S(1)}, bf16[4,48,1536]{2,1,0:T(8,128)(2,1)S(1)}, u32[]{:S(2)}, u32[]{:S(2)}) collective-permute-start(bf16[4,48,1536]{2,1,0:T(8,128)(2,1)S(1)} %shard_map.81), channel_id=1, source_target_pairs={{0,4},{4,0},{1,5},{5,1},{2,6},{6,2},{3,7},{7,3},{8,12},{12,8},{9,1... | collective-permute-start | bytes 1769480 | tf_op jit(solution)/shard_map/ppermute | solution.py:207
  21.8 1.0 %shard_map.78.mine = f32[256,1536]{1,0:T(8,128)S(1)} custom-call(f32[512,1536]{1,0:T(8,128)S(1)} %get-tuple-element.12.term, bf16[512,1024]{1,0:T(8,128)(2,1)S(1)} %get-tuple-element.13.fwd1, bf16[1024,1536]{1,0:T(8,128)(2,1)S(1)} %get-tuple-element.14.coup1), custom_call_target="tpu_custom_call" | custom-call | flops 805306368 | bytes 7340032 | tf_op jit(solution)/shard_map/pallas_call | solution.py:20
  22.8 0.0 collective-permute-done.came
  22.8 1.0 %shard_map.79 = bf16[64,16,384]{2,1,0:T(8,128)(2,1)} custom-call(f32[256,1536]{1,0:T(8,128)S(1)} %shard_map.78.mine, bf16[256,1536]{1,0:T(8,128)(2,1)S(1)} %collective-permute-done.came), custom_call_target="tpu_custom_call" | custom-call | bytes 3145728 | tf_op jit(solution)/shard_map/pallas_call | solution.py:20
  23.8 10.5 %all-to-all-start = ((bf16[64,16,384]{2,1,0:T(8,128)(2,1)}), bf16[64,16,384]{2,1,0:T(8,128)(2,1)S(1)}, u32[]{:S(2)}, u32[]{:S(2)}) async-start(bf16[64,16,384]{2,1,0:T(8,128)(2,1)} %shard_map.79), calls=%async_computation | async-start | bytes 1572864 | tf_op jit(solution)/shard_map/all_to_all | solution.py:225
  34.4 1.3 %shard_map.80.rhs = f32[16,384]{1,0:T(8,128)S(1)} custom-call(bf16[1536,512]{1,0:T(8,128)(2,1)} %rhs_hbm.1), custom_call_target="tpu_custom_call" | custom-call | bytes 1048576 | tf_op jit(solution)/shard_map/pallas_call | solution.py:20
  35.7 0.0 collective-permute-done.4
  35.7 0.2 maximum_select_fusion
  35.9 0.1 copy.8
  36.0 14.0 %all-to-all-done.parts = bf16[64,16,384]{2,1,0:T(8,128)(2,1)S(1)} async-done(((bf16[64,16,384]{2,1,0:T(8,128)(2,1)}), bf16[64,16,384]{2,1,0:T(8,128)(2,1)S(1)}, u32[]{:S(2)}, u32[]{:S(2)}) %all-to-all-start) | async-done | bytes 786464 | tf_op jit(solution)/shard_map/all_to_all | solution.py:225
  49.9 0.4 shard_map.82
  50.3 0.0 collective-permute-start.5
  50.4 2.9 %collective-permute-done.5 = f32[16,768]{1,0:T(8,128)S(1)} collective-permute-done((f32[16,768]{1,0:T(8,128)S(1)}, f32[16,768]{1,0:T(8,128)S(1)}, u32[]{:S(2)}, u32[]{:S(2)}) %collective-permute-start.5) | collective-permute-done | bytes 49184 | tf_op jit(solution)/shard_map/ppermute | solution.py:231
  53.3 0.8 collective-permute-start.6
  54.1 3.2 %collective-permute-done.6 = f32[16,384]{1,0:T(8,128)S(1)} collective-permute-done((f32[16,384]{1,0:T(8,128)S(1)}, f32[16,384]{1,0:T(8,128)S(1)}, u32[]{:S(2)}, u32[]{:S(2)}) %collective-permute-start.6) | collective-permute-done | bytes 24608 | tf_op jit(solution)/shard_map/ppermute | solution.py:233
  57.3 0.1 broadcast_in_dim.2
  57.3 16.3 %all_to_all.10.got.own = bf16[64,16,384]{2,1,0:T(8,128)(2,1)S(1)} all-to-all(bf16[64,16,384]{2,1,0:T(8,128)(2,1)S(1)} %broadcast_in_dim.2), channel_id=1, replica_groups=mesh['z'=4,'y'=4,'core'=2,'xh'=2,'xl'=2] {'z','y','xh','xl'}, dimensions={0} | all-to-all | bytes 1572864 | tf_op jit(solution)/shard_map/all_to_all | solution.py:237
  73.7 4.9 %collective-permute-start.7 = (bf16[64,16,384]{2,1,0:T(8,128)(2,1)S(1)}, bf16[64,16,384]{2,1,0:T(8,128)(2,1)S(1)}, u32[]{:S(2)}, u32[]{:S(2)}) collective-permute-start(bf16[64,16,384]{2,1,0:T(8,128)(2,1)S(1)} %all_to_all.10.got.own), channel_id=1, source_target_pairs={{0,4},{4,0},{1,5},{5,1},{2,6},{6,2},{3,7},{7,3},{8,12},{12,8},{9,1... | collective-permute-start | bytes 2359304 | tf_op jit(solution)/shard_map/ppermute | solution.py:238
  78.6 2.6 %shard_map.83 = (bf16[256,1024]{1,0:T(8,128)(2,1)S(1)}, bf16[1536,1024]{1,0:T(8,128)(2,1)S(1)}, bf16[1024,1024]{1,0:T(8,128)(2,1)S(1)}) custom-call(bf16[64,16,384]{2,1,0:T(8,128)(2,1)S(1)} %all_to_all.10.got.own, bf16[2,1536,1024]{2,1,0:T(8,128)(2,1)} %coup_hbm.5, bf16[2,1024,1024]{2,1,0:T(8,128)(2,1)} %inv_hbm.5), custom_call_target="tpu_custom_call" | custom-call | flops 805306368 | bytes 6291456 | tf_op jit(solution)/shard_map/pallas_call | solution.py:20
  81.2 0.0 collective-permute-done.7.other
  81.2 6.8 %shard_map.84 = (bf16[2,1024,512]{2,1,0:T(8,128)(2,1)}, bf16[48,512]{1,0:T(8,128)(2,1)}) custom-call(bf16[64,16,384]{2,1,0:T(8,128)(2,1)S(1)} %all_to_all.10.got.own, bf16[64,16,384]{2,1,0:T(8,128)(2,1)S(1)} %collective-permute-done.7.other, bf16[256,1024]{1,0:T(8,128)(2,1)S(1)} %get-tuple-element.18.pulled_own, ...), custom_call_target="tpu_custom_call" | custom-call | flops 3758096384 | bytes 16777216 | tf_op jit(solution)/shard_map/pallas_call | solution.py:20
  (3 shorter events, 0.0 us)
Async XLA Ops:
  0.6 9.1 %copy-start = (bf16[48,1536]{1,0:T(8,128)(2,1)S(1)}, bf16[48,1536]{1,0:T(8,128)(2,1)}, u32[]{:S(2)}) copy-start(bf16[48,1536]{1,0:T(8,128)(2,1)} %ring0.1) | copy-start | bytes 442372
  8.2 14.6 %collective-permute-start = (bf16[256,1536]{1,0:T(8,128)(2,1)S(1)}, bf16[256,1536]{1,0:T(8,128)(2,1)S(1)}, u32[]{:S(2)}, u32[]{:S(2)}) collective-permute-start(bf16[256,1536]{1,0:T(8,128)(2,1)S(1)} %get-tuple-element.15), channel_id=1, source_target_pairs={{0,4},{4,0},{1,5},{5,1},{2,6},{6,2},{3,7},{7,3},{8,12},{12,8},{9,1... | collective-permute-start | bytes 2359304 | tf_op jit(solution)/shard_map/ppermute | solution.py:222
  9.7 6.9 %collective-permute-start.1 = (bf16[48,1536]{1,0:T(8,128)(2,1)S(1)}, bf16[48,1536]{1,0:T(8,128)(2,1)S(1)}, u32[]{:S(2)}, u32[]{:S(2)}) collective-permute-start(bf16[48,1536]{1,0:T(8,128)(2,1)S(1)} %copy-done), channel_id=1, source_target_pairs={{0,8},{8,16},{16,24},{24,0},{1,9},{9,17},{17,25},{25,1},{2,10},{10... | collective-permute-start | bytes 442376 | tf_op jit(solution)/shard_map/ppermute | solution.py:205
  11.1 9.6 %collective-permute-start.2 = (bf16[48,1536]{1,0:T(8,128)(2,1)S(1)}, bf16[48,1536]{1,0:T(8,128)(2,1)S(1)}, u32[]{:S(2)}, u32[]{:S(2)}) collective-permute-start(bf16[48,1536]{1,0:T(8,128)(2,1)S(1)} %copy-done), channel_id=1, source_target_pairs={{0,16},{8,24},{16,0},{24,8},{1,17},{9,25},{17,1},{25,9},{2,18},{10... | collective-permute-start | bytes 442376 | tf_op jit(solution)/shard_map/ppermute | solution.py:205
  13.7 7.0 %collective-permute-start.3 = (bf16[48,1536]{1,0:T(8,128)(2,1)S(1)}, bf16[48,1536]{1,0:T(8,128)(2,1)S(1)}, u32[]{:S(2)}, u32[]{:S(2)}) collective-permute-start(bf16[48,1536]{1,0:T(8,128)(2,1)S(1)} %copy-done), channel_id=1, source_target_pairs={{0,24},{8,0},{16,8},{24,16},{1,25},{9,1},{17,9},{25,17},{2,26},{10... | collective-permute-start | bytes 442376 | tf_op jit(solution)/shard_map/ppermute | solution.py:205
  20.8 14.9 %collective-permute-start.4 = (bf16[4,48,1536]{2,1,0:T(8,128)(2,1)S(1)}, bf16[4,48,1536]{2,1,0:T(8,128)(2,1)S(1)}, u32[]{:S(2)}, u32[]{:S(2)}) collective-permute-start(bf16[4,48,1536]{2,1,0:T(8,128)(2,1)S(1)} %shard_map.81), channel_id=1, source_target_pairs={{0,4},{4,0},{1,5},{5,1},{2,6},{6,2},{3,7},{7,3},{8,12},{12,8},{9,1... | collective-permute-start | bytes 1769480 | tf_op jit(solution)/shard_map/ppermute | solution.py:207
  23.8 26.1 %all-to-all-start = ((bf16[64,16,384]{2,1,0:T(8,128)(2,1)}), bf16[64,16,384]{2,1,0:T(8,128)(2,1)S(1)}, u32[]{:S(2)}, u32[]{:S(2)}) async-start(bf16[64,16,384]{2,1,0:T(8,128)(2,1)} %shard_map.79), calls=%async_computation | async-start | bytes 1572864 | tf_op jit(solution)/shard_map/all_to_all | solution.py:225
  50.3 3.0 %collective-permute-start.5 = (f32[16,768]{1,0:T(8,128)S(1)}, f32[16,768]{1,0:T(8,128)S(1)}, u32[]{:S(2)}, u32[]{:S(2)}) collective-permute-start(f32[16,768]{1,0:T(8,128)S(1)} %get-tuple-element.17), channel_id=1, source_target_pairs={{0,32},{32,0},{64,96},{96,64},{1,33},{33,1},{65,97},{97,65},{2,34}... | collective-permute-start | bytes 147464 | tf_op jit(solution)/shard_map/ppermute | solution.py:231
  53.3 4.0 %collective-permute-start.6 = (f32[16,384]{1,0:T(8,128)S(1)}, f32[16,384]{1,0:T(8,128)S(1)}, u32[]{:S(2)}, u32[]{:S(2)}) collective-permute-start(f32[16,384]{1,0:T(8,128)S(1)} %constant_dynamic-slice_fusion), channel_id=1, source_target_pairs={{0,96},{96,0},{32,64},{64,32},{1,97},{97,1},{33,65},{65,33},{2,98}... | collective-permute-start | bytes 73736 | tf_op jit(solution)/shard_map/ppermute | solution.py:233
  73.7 7.5 %collective-permute-start.7 = (bf16[64,16,384]{2,1,0:T(8,128)(2,1)S(1)}, bf16[64,16,384]{2,1,0:T(8,128)(2,1)S(1)}, u32[]{:S(2)}, u32[]{:S(2)}) collective-permute-start(bf16[64,16,384]{2,1,0:T(8,128)(2,1)S(1)} %all_to_all.10.got.own), channel_id=1, source_target_pairs={{0,4},{4,0},{1,5},{5,1},{2,6},{6,2},{3,7},{7,3},{8,12},{12,8},{9,1... | collective-permute-start | bytes 2359304 | tf_op jit(solution)/shard_map/ppermute | solution.py:238

commit v6 on v5

--- a/solution.py
+++ b/solution.py
@@ -42,37 +42,42 @@
     return pl.ds(pl.multiple_of(index * size, 128), size)
 
 
-def forward_kernel(sens_hbm, inv_hbm, coup_hbm, fwd_hbm, fwd1, away, term, coup1, inv, sens, turned, coup0, fwd0, sems):
+def forward_kernel(sens_hbm, inv_hbm, coup_hbm, fwd_hbm, fwd, away, coup0, coup1, inv, sens, turned, total, sems):
     half = away.shape[0]
-    core = lax.axis_index("core")
-    fwd, coup = (fwd0, fwd1), (coup0, coup1)
+    cut = coup1.shape[0] // 2
+    core = lax.axis_index("core")
+    far = lanes(1 - core, half)
     sens_loads = [pltpu.make_async_copy(sens_hbm.at[b], sens.at[b], sems.at[b]) for b in range(2)]
     inv_loads = [pltpu.make_async_copy(inv_hbm.at[b], inv.at[b], sems.at[2 + b]) for b in range(2)]
-    coup_loads = [pltpu.make_async_copy(coup_hbm.at[b], coup[b], sems.at[4 + b]) for b in range(2)]
-    for load in (sens_loads[0], inv_loads[0], sens_loads[1], coup_loads[0], inv_loads[1], coup_loads[1]):
+    coup_load = pltpu.make_async_copy(coup_hbm.at[0], coup0, sems.at[4])
+    spans = [slice(0, cut), slice(cut, 2 * cut)]
+    last_loads = [pltpu.make_async_copy(coup_hbm.at[1, s, :], coup1.at[s, :], sems.at[5 + i]) for i, s in enumerate(spans)]
+    for load in (sens_loads[0], inv_loads[0], sens_loads[1], coup_load, inv_loads[1], *last_loads):
         load.start()
-    stores = [pltpu.make_async_copy(fwd[b], fwd_hbm.at[b], sems.at[6 + b]) for b in range(2)]
+    stores = [pltpu.make_async_copy(fwd.at[b], fwd_hbm.at[b], sems.at[7 + b]) for b in range(2)]
     sens_loads[0].wait()
     turned[0] = sens[0].T
     inv_loads[0].wait()
     sens_loads[1].wait()
-    fwd0[...] = dot(turned[0], inv[0]).astype(BF16)
+    fwd[0] = dot(turned[0], inv[0]).astype(BF16)
     turned[1] = sens[1].T
-    coup_loads[0].wait()
-    term[...] = dot(fwd0[...], coup0[...])
+    coup_load.wait()
+    total[...] = dot(fwd[0, far, :], coup0[...])
     inv_loads[1].wait()
     stores[0].start()
-    fwd1[...] = dot(turned[1], inv[1]).astype(BF16)
-    coup_loads[1].wait()
+    fwd[1] = dot(turned[1], inv[1]).astype(BF16)
+    last_loads[0].wait()
     stores[1].start()
-    away[...] = (term[lanes(1 - core, half), :] + dot(fwd1[lanes(1 - core, half), :], coup1[...])).astype(BF16)
+    total[...] += dot(fwd[1, far, spans[0]], coup1[spans[0], :])
+    last_loads[1].wait()
+    away[...] = (total[...] + dot(fwd[1, far, spans[1]], coup1[spans[1], :])).astype(BF16)
     for store in stores:
         store.wait()
 
 
-def mine_kernel(term, fwd1, coup1, out):
+def mine_kernel(fwd, coup0, coup1, out):
     rows = lanes(lax.axis_index("core"), out.shape[0])
-    out[...] = term[rows, :] + dot(fwd1[rows, :], coup1[...])
+    out[...] = dot(fwd[0, rows, :], coup0[...]) + dot(fwd[1, rows, :], coup1[...])
 
 
 def order_kernel(ring0, ring1, ring2, ring3, out):
@@ -207,20 +212,14 @@
     other = lax.ppermute(ring, "core", SWAP)
     plane = jnp.where(core == 0, jnp.stack([ring, other], 1), jnp.stack([other, ring], 1)).reshape(quarter, link)
 
-    fwd, fwd1, away, term, coup1 = call(
+    fwd, fwd_near, away, coup0, coup1 = call(
         forward_kernel,
-        (
-            pltpu.HBM((2, cols, n), BF16), pltpu.VMEM((cols, n), BF16), pltpu.VMEM((half, link), BF16),
-            pltpu.VMEM((cols, link), F32), pltpu.VMEM((n, link), BF16),
-        ),
+        (pltpu.HBM((2, cols, n), BF16), pltpu.VMEM((2, cols, n), BF16), pltpu.VMEM((half, link), BF16)) + (pltpu.VMEM((n, link), BF16),) * 2,
         [HBM] * 3, (sensitivities, block_inverse, coupling_in),
-        [
-            pltpu.VMEM((2, n, n), BF16), pltpu.VMEM((2, n, cols), BF16), pltpu.VMEM((2, cols, n), BF16), pltpu.VMEM((n, link), BF16),
-            pltpu.VMEM((cols, n), BF16), sem((8,)),
-        ],
-        24, 4 * n * cols * (n + link), 17)
+        [pltpu.VMEM((2, n, n), BF16), pltpu.VMEM((2, n, cols), BF16), pltpu.VMEM((2, cols, n), BF16), pltpu.VMEM((half, link), F32), sem((9,))],
+        24, 4 * n * cols * (n + link // 2), 17)
     came = lax.ppermute(away, "core", SWAP)
-    mine, = call(mine_kernel, (pltpu.VMEM((half, link), F32),), [VMEM] * 3, (term, fwd1, coup1), (), 8, 2 * n * half * link, 7)
+    mine, = call(mine_kernel, (pltpu.VMEM((half, link), F32),), [VMEM] * 3, (fwd_near, coup0, coup1), (), 8, 4 * n * half * link, 9)
     terms, = call(join_kernel, (pltpu.VMEM((64, piece, quarter), BF16),), [VMEM] * 2, (mine, came), (), 4, 0, 3)
     parts = lax.all_to_all(terms, CHIPS, 0, 0, tiled=True)
     rhs, = call(
@@ -237,13 +236,13 @@
     own = lax.all_to_all(spread, CHIPS, 0, 0, tiled=True)
     other = lax.ppermute(own, "core", SWAP)
 
-    pulled, coup0, inv0 = call(
+    pulled, pull0, inv0 = call(
         own_kernel, (pltpu.VMEM((half, n), BF16), pltpu.VMEM((link, n), BF16), pltpu.VMEM((n, n), BF16)),
         [VMEM] + [HBM] * 2, (own, coupling_out, block_inverse),
         [pltpu.VMEM((cols, link), BF16), pltpu.VMEM((half, n), F32), sem((4,))], 8, 2 * half * n * link, 6)
     return call(
         other_kernel, (pltpu.HBM((2, n, cols), BF16), pltpu.HBM((rows, cols), BF16)), [VMEM] * 5 + [HBM] * 3,
-        (own, other, pulled, coup0, inv0, coupling_out, block_inverse, fwd),
+        (own, other, pulled, pull0, inv0, coupling_out, block_inverse, fwd),
         [
             pltpu.VMEM((link, n), BF16), pltpu.VMEM((n, n), BF16), pltpu.VMEM((2, cols, n), BF16), pltpu.VMEM((2, n, cols), BF16),
             pltpu.VMEM((rows, cols), BF16), pltpu.VMEM((cols, link), BF16), pltpu.VMEM((2, cols, n), BF16), pltpu.VMEM((cols, n), BF16), sem((13,)),

time: 88.5 us -> 88.5 us (level)
  transfers between devices with their start and end apart: 9 -> 9, of which waited for: 5 -> 5; matrix products, arithmetic and copies ran while one was open for 0% -> 0% of each run, Pallas kernels for 7% -> 8%
where the time goes in v6:
time: 88.5 us; the launch traced here: 88.2 us
  waiting for transfers between devices  26 us (29%)
  starting transfers between devices  23.8 us (27%)
  Pallas kernels  20.7 us (23%)
  blocking collectives  16.3 us (18%)
  between operations  0.94 us (1%)
    pallas_call x8, Pallas kernels, call(): pl.pallas_call(kernel, out_shape=outs, in_specs=ins, out_specs=[VMEM if s...  20.7 us
    all_to_all x1, blocking collectives, steps(): own = lax.all_to_all(spread, CHIPS, 0, 0, tiled=True)  16.3 us
    all_to_all x1, waiting for transfers between devices, steps(): parts = lax.all_to_all(terms, CHIPS, 0, 0, tiled=True)  14 us
    all_to_all x1, starting transfers between devices, steps(): parts = lax.all_to_all(terms, CHIPS, 0, 0, tiled=True)  10.5 us
    ppermute x3, waiting for transfers between devices, steps(): lax.ppermute(border_inverse, 'y', [(i, (i + step) % 4) for i in range(4)])  5.94 us
    ppermute x3, starting transfers between devices, steps(): lax.ppermute(border_inverse, 'y', [(i, (i + step) % 4) for i in range(4)])  5.1 us
    ppermute x1, starting transfers between devices, steps(): other = lax.ppermute(own, 'core', SWAP)  4.89 us
    ppermute x1, waiting for transfers between devices, steps(): lax.ppermute(lax.dynamic_slice_in_dim(share, (1 - outer) * quarter, quart...  3.19 us
  transfers between devices with their start and end apart: 9, of which 5 were waited for; matrix products, arithmetic and copies ran while one was open for 0% of the time, Pallas kernels for 8%

profile of v6, /device:TPU:1, one launch (start us, length us, event | category | flops | bytes accessed | tf_op | source)
XLA Modules:
  0.0 88.2 jit_solution(5933520523311596911)
XLA Ops:
  0.6 0.0 copy-start
  0.6 6.8 %shard_map.77 = (bf16[2,512,1024]{2,1,0:T(8,128)(2,1)}, bf16[2,512,1024]{2,1,0:T(8,128)(2,1)S(1)}, bf16[256,1536]{1,0:T(8,128)(2,1)S(1)}, bf16[1024,1536]{1,0:T(8,128)(2,1)S(1)}, bf16[1024,1536]{1,0:T(8,128)(2,1)S(1)}) custom-call(bf16[2,1024,512]{2,1,0:T(8,128)(2,1)} %sens_hbm.1, bf16[2,1024,1024]{2,1,0:T(8,128)(2,1)} %inv_hbm.5, ...), custom_call_target="tpu_custom_call" | custom-call | flops 3758096384 | bytes 17825792 | tf_op jit(solution)/shard_map/pallas_call | solution.py:20
  7.5 1.5 %collective-permute-start = (bf16[256,1536]{1,0:T(8,128)(2,1)S(1)}, bf16[256,1536]{1,0:T(8,128)(2,1)S(1)}, u32[]{:S(2)}, u32[]{:S(2)}) collective-permute-start(bf16[256,1536]{1,0:T(8,128)(2,1)S(1)} %get-tuple-element.15), channel_id=1, source_target_pairs={{0,4},{4,0},{1,5},{5,1},{2,6},{6,2},{3,7},{7,3},{8,12},{12,8},{9,1... | collective-permute-start | bytes 2359304 | tf_op jit(solution)/shard_map/ppermute | solution.py:221
  8.9 0.0 copy-done
  8.9 1.4 %collective-permute-start.1 = (bf16[48,1536]{1,0:T(8,128)(2,1)S(1)}, bf16[48,1536]{1,0:T(8,128)(2,1)S(1)}, u32[]{:S(2)}, u32[]{:S(2)}) collective-permute-start(bf16[48,1536]{1,0:T(8,128)(2,1)S(1)} %copy-done), channel_id=1, source_target_pairs={{0,8},{8,16},{16,24},{24,0},{1,9},{9,17},{17,25},{25,1},{2,10},{10... | collective-permute-start | bytes 442376 | tf_op jit(solution)/shard_map/ppermute | solution.py:210
  10.3 2.6 %collective-permute-start.2 = (bf16[48,1536]{1,0:T(8,128)(2,1)S(1)}, bf16[48,1536]{1,0:T(8,128)(2,1)S(1)}, u32[]{:S(2)}, u32[]{:S(2)}) collective-permute-start(bf16[48,1536]{1,0:T(8,128)(2,1)S(1)} %copy-done), channel_id=1, source_target_pairs={{0,16},{8,24},{16,0},{24,8},{1,17},{9,25},{17,1},{25,9},{2,18},{10... | collective-permute-start | bytes 442376 | tf_op jit(solution)/shard_map/ppermute | solution.py:210
  13.0 1.1 %collective-permute-start.3 = (bf16[48,1536]{1,0:T(8,128)(2,1)S(1)}, bf16[48,1536]{1,0:T(8,128)(2,1)S(1)}, u32[]{:S(2)}, u32[]{:S(2)}) collective-permute-start(bf16[48,1536]{1,0:T(8,128)(2,1)S(1)} %copy-done), channel_id=1, source_target_pairs={{0,24},{8,0},{16,8},{24,16},{1,25},{9,1},{17,9},{25,17},{2,26},{10... | collective-permute-start | bytes 442376 | tf_op jit(solution)/shard_map/ppermute | solution.py:210
  14.0 1.8 %collective-permute-done.1.ring1 = bf16[48,1536]{1,0:T(8,128)(2,1)S(1)} collective-permute-done((bf16[48,1536]{1,0:T(8,128)(2,1)S(1)}, bf16[48,1536]{1,0:T(8,128)(2,1)S(1)}, u32[]{:S(2)}, u32[]{:S(2)}) %collective-permute-start.1) | collective-permute-done | bytes 147488 | tf_op jit(solution)/shard_map/ppermute | solution.py:210
  15.8 4.2 %collective-permute-done.2.ring2 = bf16[48,1536]{1,0:T(8,128)(2,1)S(1)} collective-permute-done((bf16[48,1536]{1,0:T(8,128)(2,1)S(1)}, bf16[48,1536]{1,0:T(8,128)(2,1)S(1)}, u32[]{:S(2)}, u32[]{:S(2)}) %collective-permute-start.2) | collective-permute-done | bytes 147488 | tf_op jit(solution)/shard_map/ppermute | solution.py:210
  20.0 0.0 collective-permute-done.3.ring3
  20.0 0.1 shard_map.81
  20.0 1.0 %collective-permute-start.4 = (bf16[4,48,1536]{2,1,0:T(8,128)(2,1)S(1)}, bf16[4,48,1536]{2,1,0:T(8,128)(2,1)S(1)}, u32[]{:S(2)}, u32[]{:S(2)}) collective-permute-start(bf16[4,48,1536]{2,1,0:T(8,128)(2,1)S(1)} %shard_map.81), channel_id=1, source_target_pairs={{0,4},{4,0},{1,5},{5,1},{2,6},{6,2},{3,7},{7,3},{8,12},{12,8},{9,1... | collective-permute-start | bytes 1769480 | tf_op jit(solution)/shard_map/ppermute | solution.py:212
  21.1 1.8 %shard_map.78.mine = f32[256,1536]{1,0:T(8,128)S(1)} custom-call(bf16[2,512,1024]{2,1,0:T(8,128)(2,1)S(1)} %get-tuple-element.12.fwd, bf16[1024,1536]{1,0:T(8,128)(2,1)S(1)} %get-tuple-element.13.coup0, bf16[1024,1536]{1,0:T(8,128)(2,1)S(1)} %get-tuple-element.14.coup1), custom_call_target="tpu_custom_call" | custom-call | flops 1610612736 | bytes 9437184 | tf_op jit(solution)/shard_map/pallas_call | solution.py:20
  22.8 0.0 collective-permute-done.came
  22.8 1.0 %shard_map.79 = bf16[64,16,384]{2,1,0:T(8,128)(2,1)} custom-call(f32[256,1536]{1,0:T(8,128)S(1)} %shard_map.78.mine, bf16[256,1536]{1,0:T(8,128)(2,1)S(1)} %collective-permute-done.came), custom_call_target="tpu_custom_call" | custom-call | bytes 3145728 | tf_op jit(solution)/shard_map/pallas_call | solution.py:20
  23.9 10.5 %all-to-all-start = ((bf16[64,16,384]{2,1,0:T(8,128)(2,1)}), bf16[64,16,384]{2,1,0:T(8,128)(2,1)S(1)}, u32[]{:S(2)}, u32[]{:S(2)}) async-start(bf16[64,16,384]{2,1,0:T(8,128)(2,1)} %shard_map.79), calls=%async_computation | async-start | bytes 1572864 | tf_op jit(solution)/shard_map/all_to_all | solution.py:224
  34.4 1.3 %shard_map.80.rhs = f32[16,384]{1,0:T(8,128)S(1)} custom-call(bf16[1536,512]{1,0:T(8,128)(2,1)} %rhs_hbm.1), custom_call_target="tpu_custom_call" | custom-call | bytes 1048576 | tf_op jit(solution)/shard_map/pallas_call | solution.py:20
  35.7 0.0 collective-permute-done.4
  35.7 0.2 maximum_select_fusion
  35.9 0.1 copy.8
  36.0 14.0 %all-to-all-done.parts = bf16[64,16,384]{2,1,0:T(8,128)(2,1)S(1)} async-done(((bf16[64,16,384]{2,1,0:T(8,128)(2,1)}), bf16[64,16,384]{2,1,0:T(8,128)(2,1)S(1)}, u32[]{:S(2)}, u32[]{:S(2)}) %all-to-all-start) | async-done | bytes 786464 | tf_op jit(solution)/shard_map/all_to_all | solution.py:224
  50.0 0.4 shard_map.82
  50.3 0.0 collective-permute-start.5
  50.4 2.9 %collective-permute-done.5 = f32[16,768]{1,0:T(8,128)S(1)} collective-permute-done((f32[16,768]{1,0:T(8,128)S(1)}, f32[16,768]{1,0:T(8,128)S(1)}, u32[]{:S(2)}, u32[]{:S(2)}) %collective-permute-start.5) | collective-permute-done | bytes 49184 | tf_op jit(solution)/shard_map/ppermute | solution.py:230
  53.3 0.8 collective-permute-start.6
  54.1 3.2 %collective-permute-done.6 = f32[16,384]{1,0:T(8,128)S(1)} collective-permute-done((f32[16,384]{1,0:T(8,128)S(1)}, f32[16,384]{1,0:T(8,128)S(1)}, u32[]{:S(2)}, u32[]{:S(2)}) %collective-permute-start.6) | collective-permute-done | bytes 24608 | tf_op jit(solution)/shard_map/ppermute | solution.py:232
  57.3 0.1 broadcast_in_dim.2
  57.4 16.3 %all_to_all.10.got.own = bf16[64,16,384]{2,1,0:T(8,128)(2,1)S(1)} all-to-all(bf16[64,16,384]{2,1,0:T(8,128)(2,1)S(1)} %broadcast_in_dim.2), channel_id=1, replica_groups=mesh['z'=4,'y'=4,'core'=2,'xh'=2,'xl'=2] {'z','y','xh','xl'}, dimensions={0} | all-to-all | bytes 1572864 | tf_op jit(solution)/shard_map/all_to_all | solution.py:236
  73.7 4.9 %collective-permute-start.7 = (bf16[64,16,384]{2,1,0:T(8,128)(2,1)S(1)}, bf16[64,16,384]{2,1,0:T(8,128)(2,1)S(1)}, u32[]{:S(2)}, u32[]{:S(2)}) collective-permute-start(bf16[64,16,384]{2,1,0:T(8,128)(2,1)S(1)} %all_to_all.10.got.own), channel_id=1, source_target_pairs={{0,4},{4,0},{1,5},{5,1},{2,6},{6,2},{3,7},{7,3},{8,12},{12,8},{9,1... | collective-permute-start | bytes 2359304 | tf_op jit(solution)/shard_map/ppermute | solution.py:237
  78.6 2.6 %shard_map.83 = (bf16[256,1024]{1,0:T(8,128)(2,1)S(1)}, bf16[1536,1024]{1,0:T(8,128)(2,1)S(1)}, bf16[1024,1024]{1,0:T(8,128)(2,1)S(1)}) custom-call(bf16[64,16,384]{2,1,0:T(8,128)(2,1)S(1)} %all_to_all.10.got.own, bf16[2,1536,1024]{2,1,0:T(8,128)(2,1)} %coup_hbm.5, bf16[2,1024,1024]{2,1,0:T(8,128)(2,1)} %inv_hbm.5), custom_call_target="tpu_custom_call" | custom-call | flops 805306368 | bytes 6291456 | tf_op jit(solution)/shard_map/pallas_call | solution.py:20
  81.2 0.0 collective-permute-done.7.other
  81.2 6.8 %shard_map.84 = (bf16[2,1024,512]{2,1,0:T(8,128)(2,1)}, bf16[48,512]{1,0:T(8,128)(2,1)}) custom-call(bf16[64,16,384]{2,1,0:T(8,128)(2,1)S(1)} %all_to_all.10.got.own, bf16[64,16,384]{2,1,0:T(8,128)(2,1)S(1)} %collective-permute-done.7.other, bf16[256,1024]{1,0:T(8,128)(2,1)S(1)} %get-tuple-element.18.pulled_own, ...), custom_call_target="tpu_custom_call" | custom-call | flops 3758096384 | bytes 16777216 | tf_op jit(solution)/shard_map/pallas_call | solution.py:20
  (3 shorter events, 0.0 us)
Async XLA Ops:
  0.6 8.3 %copy-start = (bf16[48,1536]{1,0:T(8,128)(2,1)S(1)}, bf16[48,1536]{1,0:T(8,128)(2,1)}, u32[]{:S(2)}) copy-start(bf16[48,1536]{1,0:T(8,128)(2,1)} %ring0.1) | copy-start | bytes 442372
  7.5 15.4 %collective-permute-start = (bf16[256,1536]{1,0:T(8,128)(2,1)S(1)}, bf16[256,1536]{1,0:T(8,128)(2,1)S(1)}, u32[]{:S(2)}, u32[]{:S(2)}) collective-permute-start(bf16[256,1536]{1,0:T(8,128)(2,1)S(1)} %get-tuple-element.15), channel_id=1, source_target_pairs={{0,4},{4,0},{1,5},{5,1},{2,6},{6,2},{3,7},{7,3},{8,12},{12,8},{9,1... | collective-permute-start | bytes 2359304 | tf_op jit(solution)/shard_map/ppermute | solution.py:221
  8.9 6.9 %collective-permute-start.1 = (bf16[48,1536]{1,0:T(8,128)(2,1)S(1)}, bf16[48,1536]{1,0:T(8,128)(2,1)S(1)}, u32[]{:S(2)}, u32[]{:S(2)}) collective-permute-start(bf16[48,1536]{1,0:T(8,128)(2,1)S(1)} %copy-done), channel_id=1, source_target_pairs={{0,8},{8,16},{16,24},{24,0},{1,9},{9,17},{17,25},{25,1},{2,10},{10... | collective-permute-start | bytes 442376 | tf_op jit(solution)/shard_map/ppermute | solution.py:210
  10.3 9.6 %collective-permute-start.2 = (bf16[48,1536]{1,0:T(8,128)(2,1)S(1)}, bf16[48,1536]{1,0:T(8,128)(2,1)S(1)}, u32[]{:S(2)}, u32[]{:S(2)}) collective-permute-start(bf16[48,1536]{1,0:T(8,128)(2,1)S(1)} %copy-done), channel_id=1, source_target_pairs={{0,16},{8,24},{16,0},{24,8},{1,17},{9,25},{17,1},{25,9},{2,18},{10... | collective-permute-start | bytes 442376 | tf_op jit(solution)/shard_map/ppermute | solution.py:210
  13.0 7.0 %collective-permute-start.3 = (bf16[48,1536]{1,0:T(8,128)(2,1)S(1)}, bf16[48,1536]{1,0:T(8,128)(2,1)S(1)}, u32[]{:S(2)}, u32[]{:S(2)}) collective-permute-start(bf16[48,1536]{1,0:T(8,128)(2,1)S(1)} %copy-done), channel_id=1, source_target_pairs={{0,24},{8,0},{16,8},{24,16},{1,25},{9,1},{17,9},{25,17},{2,26},{10... | collective-permute-start | bytes 442376 | tf_op jit(solution)/shard_map/ppermute | solution.py:210
  20.0 15.7 %collective-permute-start.4 = (bf16[4,48,1536]{2,1,0:T(8,128)(2,1)S(1)}, bf16[4,48,1536]{2,1,0:T(8,128)(2,1)S(1)}, u32[]{:S(2)}, u32[]{:S(2)}) collective-permute-start(bf16[4,48,1536]{2,1,0:T(8,128)(2,1)S(1)} %shard_map.81), channel_id=1, source_target_pairs={{0,4},{4,0},{1,5},{5,1},{2,6},{6,2},{3,7},{7,3},{8,12},{12,8},{9,1... | collective-permute-start | bytes 1769480 | tf_op jit(solution)/shard_map/ppermute | solution.py:212
  23.9 26.1 %all-to-all-start = ((bf16[64,16,384]{2,1,0:T(8,128)(2,1)}), bf16[64,16,384]{2,1,0:T(8,128)(2,1)S(1)}, u32[]{:S(2)}, u32[]{:S(2)}) async-start(bf16[64,16,384]{2,1,0:T(8,128)(2,1)} %shard_map.79), calls=%async_computation | async-start | bytes 1572864 | tf_op jit(solution)/shard_map/all_to_all | solution.py:224
  50.3 3.0 %collective-permute-start.5 = (f32[16,768]{1,0:T(8,128)S(1)}, f32[16,768]{1,0:T(8,128)S(1)}, u32[]{:S(2)}, u32[]{:S(2)}) collective-permute-start(f32[16,768]{1,0:T(8,128)S(1)} %get-tuple-element.17), channel_id=1, source_target_pairs={{0,32},{32,0},{64,96},{96,64},{1,33},{33,1},{65,97},{97,65},{2,34}... | collective-permute-start | bytes 147464 | tf_op jit(solution)/shard_map/ppermute | solution.py:230
  53.3 4.0 %collective-permute-start.6 = (f32[16,384]{1,0:T(8,128)S(1)}, f32[16,384]{1,0:T(8,128)S(1)}, u32[]{:S(2)}, u32[]{:S(2)}) collective-permute-start(f32[16,384]{1,0:T(8,128)S(1)} %constant_dynamic-slice_fusion), channel_id=1, source_target_pairs={{0,96},{96,0},{32,64},{64,32},{1,97},{97,1},{33,65},{65,33},{2,98}... | collective-permute-start | bytes 73736 | tf_op jit(solution)/shard_map/ppermute | solution.py:232
  73.7 7.5 %collective-permute-start.7 = (bf16[64,16,384]{2,1,0:T(8,128)(2,1)S(1)}, bf16[64,16,384]{2,1,0:T(8,128)(2,1)S(1)}, u32[]{:S(2)}, u32[]{:S(2)}) collective-permute-start(bf16[64,16,384]{2,1,0:T(8,128)(2,1)S(1)} %all_to_all.10.got.own), channel_id=1, source_target_pairs={{0,4},{4,0},{1,5},{5,1},{2,6},{6,2},{3,7},{7,3},{8,12},{12,8},{9,1... | collective-permute-start | bytes 2359304 | tf_op jit(solution)/shard_map/ppermute | solution.py:237
